TPU v7x, 32 devices: a whole 2x2x4 slice. The times are simulated.
32 devices in a mesh: frame: 2 (over x), tile: 16 (over z, y, core).
Axes of the slice: x: 2, y: 2, z: 4, core: 2. Of those that a mesh axis runs over, the one named last changes fastest.
Arguments:
- latents: bfloat16 [4, 64, 128, 512], P('frame', 'tile'), may hold values from -6 to 6
- conv_weight: bfloat16 [3, 3, 512, 512], replicated, may hold values from -0.09375 to 0.09375
- conv_bias: float32 [512], replicated, may hold values from -3 to 3
- query_weight: bfloat16 [512, 512], replicated, may hold values from -0.176776695 to 0.176776695
- key_weight: bfloat16 [512, 512], replicated, may hold values from -8 to 8
- value_weight: bfloat16 [512, 512], replicated, may hold values from -0.25 to 0.25
- out_weight: bfloat16 [512, 512], replicated, may hold values from -0.25 to 0.25
- cotangent: bfloat16 [4, 64, 128, 512], P('frame', 'tile'), may hold values from -0.032958984 to 0.032958984
Outputs:
- mixed_frames: bfloat16 [4, 64, 128, 512], P('frame', 'tile')
- conv_grad: float32 [512, 4608], P('tile', 'frame')
All inputs are finite; a program needn't handle non-finite values.
Results may differ from a plain program's by a relative error of at most 0.0065.
Values may be sent and summed in bfloat16 or wider, within the bound.
A program may use at most 128 MiB of HBM per device.

v0:
```python
import math

import jax
import jax.numpy as jnp
from jax import lax
from jax.sharding import PartitionSpec as P

HEADS = 8


def with_halo(cells, sides, width):
    for axis, dim in sides:
        count = lax.axis_size(axis)
        ends = count - 1
        head = lax.slice_in_dim(cells, 0, width, axis=dim)
        tail = lax.slice_in_dim(cells, cells.shape[dim] - width, cells.shape[dim], axis=dim)
        cells = jnp.concatenate(
            [
                lax.ppermute(tail, axis, [(i, (i + 1) % count) for i in range(ends)]),
                cells,
                lax.ppermute(head, axis, [((i + 1) % count, i) for i in range(ends)]),
            ],
            axis=dim,
        )
    return cells


def on_device(
    latents, conv_weight, conv_bias, query_weight, key_weight, value_weight, out_weight, cotangent
):
    channels = latents.shape[3]
    head_dim = channels // HEADS
    padded = with_halo(latents, (("tile", 1),), 1)
    convolved = lax.conv_general_dilated(
        padded,
        conv_weight,
        (1, 1),
        ((0, 0), (1, 1)),
        dimension_numbers=("NHWC", "HWIO", "NHWC"),
        preferred_element_type=jnp.float32,
    )
    hidden = jax.nn.silu(convolved + conv_bias).astype(jnp.bfloat16)
    blocked = lax.all_to_all(hidden, "frame", split_axis=2, concat_axis=0, tiled=True)
    frames, row_count, col_count, _ = blocked.shape
    tokens = blocked.reshape(-1, channels)
    queries = jnp.dot(tokens, query_weight, preferred_element_type=jnp.float32).astype(jnp.bfloat16)
    key_rows = jnp.dot(tokens, key_weight, preferred_element_type=jnp.float32).astype(jnp.bfloat16)
    values = jnp.dot(tokens, value_weight, preferred_element_type=jnp.float32).astype(jnp.bfloat16)
    shaped = (frames, row_count * col_count, HEADS, head_dim)
    queries = queries.reshape(shaped)
    key_rows = key_rows.reshape(shaped)
    values = values.reshape(shaped)
    scores = jnp.einsum(
        "fphd,gphd->phfg", queries, key_rows, preferred_element_type=jnp.float32
    ) / math.sqrt(head_dim)
    weights = jax.nn.softmax(scores, axis=-1).astype(jnp.bfloat16)
    head_out = jnp.einsum(
        "phfg,gphd->fphd", weights, values, preferred_element_type=jnp.float32
    ).astype(jnp.bfloat16)
    projected = jnp.dot(
        head_out.reshape(-1, channels), out_weight, preferred_element_type=jnp.float32
    )
    mixed_tokens = tokens.astype(jnp.float32) + projected
    pixel_mixed = mixed_tokens.astype(jnp.bfloat16).reshape(frames, row_count, col_count, channels)
    mixed_frames = lax.all_to_all(pixel_mixed, "frame", split_axis=0, concat_axis=2, tiled=True)
    rimmed = with_halo(mixed_frames, (("tile", 1),), 1)
    widened = jnp.pad(rimmed, ((0, 0), (0, 0), (1, 1), (0, 0)))
    row_count = mixed_frames.shape[1]
    col_count = mixed_frames.shape[2]
    pieces = []
    for row_shift in range(3):
        for col_shift in range(3):
            pieces.append(
                widened[
                    :, row_shift : row_shift + row_count, col_shift : col_shift + col_count, :
                ].reshape(-1, channels)
            )
    patches = jnp.concatenate(pieces, axis=1)
    flat_cot = cotangent.reshape(-1, channels)
    partial_grad = lax.psum_scatter(
        lax.dot_general(
            flat_cot, patches, (((0,), (0,)), ((), ())), preferred_element_type=jnp.float32
        ),
        "tile",
        scatter_dimension=0,
        tiled=True,
    )
    conv_grad = lax.psum_scatter(partial_grad, "frame", scatter_dimension=1, tiled=True)
    return (mixed_frames, conv_grad)


def solution(mesh):
    in_specs = (
        P("frame", "tile", None, None),
        P(),
        P(),
        P(),
        P(),
        P(),
        P(),
        P("frame", "tile", None, None),
    )
    out_specs = (P("frame", "tile", None, None), P("tile", "frame"))
    return jax.shard_map(
        on_device, mesh=mesh, in_specs=in_specs, out_specs=out_specs, check_vma=False
    )
```

profile of v0, /device:TPU:0, one launch (start us, length us, event | category | flops | bytes accessed | tf_op | source)
XLA Modules:
  0.0 291.4 jit_solution(739361815925212230)
XLA Ops:
  7.2 1.2 fusion.27
  8.5 2.5 collective-permute-start
  11.0 1.3 collective-permute-start.1
  12.3 4.2 %collective-permute-done.1 = bf16[2,1,128,512]{3,2,1,0:T(8,128)(2,1)S(1)} collective-permute-done((bf16[2,1,128,512]{3,2,1,0:T(8,128)(2,1)S(1)}, bf16[2,1,128,512]{3,2,1,0:T(8,128)(2,1)S(1)}, u32[]{:S(2)}, u32[]{:S(2)}) %collective-permute-start.1) | collective-permute-done | bytes 262176 | tf_op jit(solution)/shard_map/ppermute | solution.py:21
  16.6 1.4 maximum_bitcast_fusion
  18.0 1.6 copy.58
  19.6 1.3 pad.5.clone
  21.0 1.7 fusion.16
  22.8 5.8 %multiply_convert_fusion = bf16[4,16,17,512]{3,1,2,0:T(8,128)(2,1)S(1)} fusion(bf16[3,3,512,512]{3,2,1,0:T(8,128)(2,1)S(1)} %bitcast.79, bf16[6,2,8,19,512]{4,1,3,2,0:T(2,128)(2,1)S(1)} %fusion.16, f32[512]{0:T(512)S(1)} %copy-done.5, pred[16,17]{0,1:T(8,128)(4,1)S(1)} %copy-done.6), kind=kOutput, calls=%fused_computation.10 | convolution fusion | flops 5137727488 | bytes 7702800 | tf_op jit(solution)/shard_map/conv_general_dilated | solution.py:34
  28.5 0.9 copy.35
  30.1 13.9 %all_to_all.33 = bf16[2,4,128,512]{3,1,0,2:T(4,128)(2,1)S(1)} all-to-all(bf16[2,4,128,512]{3,1,0,2:T(4,128)(2,1)S(1)} %copy.36), channel_id=1, replica_groups=mesh['frame'=2,'tile'=16] {'frame'}, dimensions={2} | all-to-all | bytes 2097152 | tf_op jit(solution)/shard_map/all_to_all | solution.py:43
  45.8 2.1 reshape.85
  47.9 1.7 convolution_convert_fusion.1
  49.6 2.1 reshape.84
  51.7 2.7 convolution_convert_fusion.2
  54.4 2.8 reshape.83
  57.2 5.0 %fusion.5 = f32[256,8,4,4]{2,3,1,0:T(4,128)S(1)} fusion(bf16[4,256,8,64]{3,2,1,0:T(8,128)(2,1)} %reshape.85, bf16[4,256,8,64]{3,2,1,0:T(8,128)(2,1)} %reshape.84), kind=kOutput, calls=%fused_computation.11 | convolution fusion | flops 4194304 | bytes 2228224 | tf_op jit(solution)/shard_map/fphd,gphd->phfg/dot_general | solution.py:53
  62.3 6.4 %fusion.28 = (f32[256,8,4]{2,1,0:T(8,128)S(1)}, f32[256,8,4,4]{2,3,1,0:T(4,128)S(1)}) fusion(f32[256,8,4,4]{2,3,1,0:T(4,128)S(1)} %fusion.5), kind=kOutput, calls=%fused_computation.48 | output fusion | flops 131075 | bytes 294912 | tf_op jit(solution)/shard_map/sub | solution.py:56
  68.6 4.2 %convert_bitcast_fusion = bf16[4,256,8,64]{3,0,2,1:T(4,128)(2,1)} fusion(f32[256,8,4,4]{2,3,1,0:T(4,128)S(1)} %get-tuple-element.21, f32[256,8,4]{2,1,0:T(8,128)S(1)} %get-tuple-element.20, bf16[4,256,8,64]{3,2,1,0:T(8,128)(2,1)S(1)} %reshape.83), kind=kOutput, calls=%fused_computation.17 | convolution fusion | flops 4784128 | bytes 2260992 | tf_op jit(solution)/shard_map/phfg,gphd->fphd/dot_general | solution.py:57
  72.8 3.8 %copy.46 = bf16[4,256,8,64]{1,0,3,2:T(4,128)(2,1)S(1)} copy(bf16[4,256,8,64]{3,0,2,1:T(4,128)(2,1)} %convert_bitcast_fusion) | data formatting | bytes 2097152 | tf_op jit(solution)/shard_map/convert_element_type | solution.py:59
  76.8 1.8 add_convert_fusion
  78.6 14.9 %all_to_all.34 = bf16[4,4,64,512]{3,2,1,0:T(8,128)(2,1)S(1)} all-to-all(bf16[4,4,64,512]{3,2,1,0:T(8,128)(2,1)S(1)} %bitcast.77), channel_id=1, replica_groups=mesh['frame'=2,'tile'=16] {'frame'}, dimensions={0} | all-to-all | bytes 2097152 | tf_op jit(solution)/shard_map/all_to_all | solution.py:65
  93.7 4.3 %collective-permute-start.2 = (bf16[2,1,128,512]{3,2,1,0:T(8,128)(2,1)S(1)}, bf16[2,1,128,512]{3,2,1,0:T(8,128)(2,1)S(1)}, u32[]{:S(2)}, u32[]{:S(2)}) collective-permute-start(bf16[2,1,128,512]{3,2,1,0:T(8,128)(2,1)S(1)} %get-tuple-element.16), channel_id=1, source_target_pairs={{0,1},{1,2},{2,3},{3,4},{4,5},{5,6},{6,7},{7,8},{8,9},{9,10},{10,1... | collective-permute-start | bytes 786440 | tf_op jit(solution)/shard_map/ppermute | solution.py:19
  98.0 1.3 collective-permute-start.3
  99.3 8.0 %collective-permute-done.3 = bf16[2,1,128,512]{3,2,1,0:T(8,128)(2,1)S(1)} collective-permute-done((bf16[2,1,128,512]{3,2,1,0:T(8,128)(2,1)S(1)}, bf16[2,1,128,512]{3,2,1,0:T(8,128)(2,1)S(1)}, u32[]{:S(2)}, u32[]{:S(2)}) %collective-permute-start.3) | collective-permute-done | bytes 262176 | tf_op jit(solution)/shard_map/ppermute | solution.py:21
  107.7 0.9 fusion.25
  109.5 7.5 %convolution_bitcast_fusion = f32[512,4608]{0,1:T(8,128)} fusion(bf16[1024,4608]{1,0:T(8,128)(2,1)S(1)} %constant_dynamic-update-slice_fusion, bf16[1024,512]{1,0:T(8,128)(2,1)S(1)} %bitcast.52), kind=kOutput, calls=%fused_computation.1 | convolution fusion | flops 4831838208 | bytes 19922944 | tf_op jit(solution)/shard_map/dot_general | solution.py:81
  117.1 9.6 %copy.56 = f32[512,4608]{1,0:T(8,128)} copy(f32[512,4608]{0,1:T(8,128)} %convolution_bitcast_fusion) | data formatting | bytes 18874368
  126.7 117.7 %reduce-scatter.7.cloned.1.call-done = f32[32,4608]{1,0:T(8,128)} async-done(((f32[512,4608]{1,0:T(8,128)}), f32[32,4608]{1,0:T(8,128)}) %reduce-scatter.7.cloned.1.call-update) | async-done | bytes 589840
  244.5 3.2 %copy.57 = f32[32,4608]{0,1:T(8,128)} copy(f32[32,4608]{1,0:T(8,128)} %reduce-scatter.7.cloned.1.call-done) | data formatting | bytes 1179648
  247.7 34.6 %reduce-scatter.5.cloned.1.call-done = f32[32,2304]{0,1:T(8,128)} async-done(((f32[32,4608]{0,1:T(8,128)}), f32[32,2304]{0,1:T(8,128)}) %reduce-scatter.5.cloned.1.call-update) | async-done | bytes 294928 | tf_op jit(solution)/shard_map/reduce_scatter | solution.py:88
  282.3 2.3 copy.48
  (45 shorter events, 4.3 us)
Async XLA Ops:
  7.2 102.4 %copy-start = (bf16[2,4,128,512]{3,2,1,0:T(8,128)(2,1)S(1)}, bf16[2,4,128,512]{3,2,1,0:T(8,128)(2,1)}, u32[]{:S(2)}) copy-start(bf16[2,4,128,512]{3,2,1,0:T(8,128)(2,1)} %param.15) | copy-start | bytes 3145732
  7.2 237.3 %reduce-scatter.7.cloned.1.call-start = ((), (), s32[]{:S(2)}) async-start(), calls=%async_computation.5 | async-start | bytes 10027008
  7.2 15.5 %slice-start = ((s8[4718592]{0:T(1024)(128)(4,1)}), s8[4194304]{0:T(1024)(128)(4,1)S(1)}, s32[]{:S(2)}) async-start(s8[4718592]{0:T(1024)(128)(4,1)} %bitcast.78), calls=%async_computation.6 | async-start | bytes 8388608
  8.5 3.9 %collective-permute-start = (bf16[2,1,128,512]{3,2,1,0:T(8,128)(2,1)S(1)}, bf16[2,1,128,512]{3,2,1,0:T(8,128)(2,1)S(1)}, u32[]{:S(2)}, u32[]{:S(2)}) collective-permute-start(bf16[2,1,128,512]{3,2,1,0:T(8,128)(2,1)S(1)} %get-tuple-element.18), channel_id=1, source_target_pairs={{0,1},{1,2},{2,3},{3,4},{4,5},{5,6},{6,7},{7,8},{8,9},{9,10},{10,1... | collective-permute-start | bytes 786440 | tf_op jit(solution)/shard_map/ppermute | solution.py:19
  11.0 5.5 %collective-permute-start.1 = (bf16[2,1,128,512]{3,2,1,0:T(8,128)(2,1)S(1)}, bf16[2,1,128,512]{3,2,1,0:T(8,128)(2,1)S(1)}, u32[]{:S(2)}, u32[]{:S(2)}) collective-permute-start(bf16[2,1,128,512]{3,2,1,0:T(8,128)(2,1)S(1)} %get-tuple-element.19), channel_id=1, source_target_pairs={{1,0},{2,1},{3,2},{4,3},{5,4},{6,5},{7,6},{8,7},{9,8},{10,9},{11,1... | collective-permute-start | bytes 786440 | tf_op jit(solution)/shard_map/ppermute | solution.py:21
  18.0 4.8 %slice-start.1 = ((s8[4718592]{0:T(1024)(128)(4,1)}), s8[524288]{0:T(1024)(128)(4,1)S(1)}, s32[]{:S(2)}) async-start(s8[4718592]{0:T(1024)(128)(4,1)} %bitcast.78), calls=%async_computation.7 | async-start | bytes 1048576
  20.9 1.9 copy-start.5
  20.9 1.9 copy-start.6
  44.0 1.0 copy-start.4
  44.4 7.3 %copy-start.2 = (bf16[2,2,4,64,512]{4,3,2,1,0:T(8,128)(2,1)}, bf16[2,2,4,64,512]{4,3,2,1,0:T(8,128)(2,1)S(1)}, u32[]{:S(2)}) copy-start(bf16[2,2,4,64,512]{4,3,2,1,0:T(8,128)(2,1)S(1)} %copy.38) | copy-start | bytes 3145732
  72.8 4.0 %copy-start.3 = (bf16[2,2,4,64,512]{4,3,2,1,0:T(8,128)(2,1)S(1)}, bf16[2,2,4,64,512]{4,3,2,1,0:T(8,128)(2,1)}, u32[]{:S(2)}) copy-start(bf16[2,2,4,64,512]{4,3,2,1,0:T(8,128)(2,1)} %copy-done.2) | copy-start | bytes 3145732
  93.6 15.5 %copy-start.1 = (bf16[2,2,4,64,512]{4,3,0,2,1:T(8,128)(2,1)}, bf16[2,2,4,64,512]{4,3,0,2,1:T(8,128)(2,1)S(1)}, u32[]{:S(2)}) copy-start(bf16[2,2,4,64,512]{4,3,0,2,1:T(8,128)(2,1)S(1)} %copy.47) | copy-start | bytes 3145732
  93.7 5.6 %collective-permute-start.2 = (bf16[2,1,128,512]{3,2,1,0:T(8,128)(2,1)S(1)}, bf16[2,1,128,512]{3,2,1,0:T(8,128)(2,1)S(1)}, u32[]{:S(2)}, u32[]{:S(2)}) collective-permute-start(bf16[2,1,128,512]{3,2,1,0:T(8,128)(2,1)S(1)} %get-tuple-element.16), channel_id=1, source_target_pairs={{0,1},{1,2},{2,3},{3,4},{4,5},{5,6},{6,7},{7,8},{8,9},{9,10},{10,1... | collective-permute-start | bytes 786440 | tf_op jit(solution)/shard_map/ppermute | solution.py:19
  98.0 9.3 %collective-permute-start.3 = (bf16[2,1,128,512]{3,2,1,0:T(8,128)(2,1)S(1)}, bf16[2,1,128,512]{3,2,1,0:T(8,128)(2,1)S(1)}, u32[]{:S(2)}, u32[]{:S(2)}) collective-permute-start(bf16[2,1,128,512]{3,2,1,0:T(8,128)(2,1)S(1)} %get-tuple-element.17), channel_id=1, source_target_pairs={{1,0},{2,1},{3,2},{4,3},{5,4},{6,5},{7,6},{8,7},{9,8},{10,9},{11,1... | collective-permute-start | bytes 786440 | tf_op jit(solution)/shard_map/ppermute | solution.py:21
  126.7 155.6 %reduce-scatter.5.cloned.1.call-start = ((), (), s32[]{:S(2)}) async-start(), calls=%async_computation.4 | async-start | bytes 3538944 | tf_op jit(solution)/shard_map/reduce_scatter | solution.py:88
Sparse Core Ops, SparseCore 0:
  126.8 117.6 reduce-scatter.6
  247.8 34.4 reduce-scatter.4
where the time goes:
time: 292 us; the launch traced here: 291 us
  waiting for transfers between devices  165 us (57%)
  local copies, waits for them, and re-layouts  34.6 us (12%)
  matrix products  29.5 us (10%)
  blocking collectives  28.8 us (10%)
  between operations  14.5 us (5%)
  other arithmetic  10.1 us (3%)
  starting transfers between devices  9.5 us (3%)
    unnamed x3, waiting for transfers between devices  118 us
    reduce_scatter x1, waiting for transfers between devices, on_device(): lax.psum_scatter(partial_grad, 'frame', scatter_dimension=1, tiled=True)  34.6 us
    unnamed x31, local copies, waits for them, and re-layouts  18.2 us
    all_to_all x1, blocking collectives, on_device(): lax.all_to_all(pixel_mixed, 'frame', split_axis=0, concat_axis=2, tiled=T...  14.9 us
    all_to_all x1, blocking collectives, on_device(): lax.all_to_all(hidden, 'frame', split_axis=2, concat_axis=0, tiled=True)  13.9 us
    ppermute x2, waiting for transfers between devices, with_halo(): lax.ppermute(head, axis, [((i + 1) % count, i) for i in range(ends)])  12.2 us
    dot_general x1, matrix products, on_device(): lax.dot_general(flat_cot, patches, (((0,), (0,)), ((), ())), preferred_el...  7.55 us
    ppermute x2, starting transfers between devices, with_halo(): lax.ppermute(tail, axis, [(i, (i + 1) % count) for i in range(ends)])  6.84 us
  transfers between devices with their start and end apart: 6, of which 4 were waited for; matrix products, arithmetic and copies ran while one was open for 0% of the time, Pallas kernels for 0%

commit v1 on v0

v1 whole, which is shorter than its diff:
```python
import functools
import math

import jax
import jax.numpy as jnp
from jax import lax
from jax.experimental import pallas as pl
from jax.experimental.pallas import tpu as pltpu
from jax.sharding import PartitionSpec as P

HEADS = 8
LANES = 128
MESH = pl.DeviceIdType.MESH
F32 = jnp.float32
BF16 = jnp.bfloat16


def with_halo(cells, axis, dim):
    count = lax.axis_size(axis)
    ends = count - 1
    head = lax.slice_in_dim(cells, 0, 1, axis=dim)
    tail = lax.slice_in_dim(cells, cells.shape[dim] - 1, cells.shape[dim], axis=dim)
    return jnp.concatenate(
        [
            lax.ppermute(tail, axis, [(i, i + 1) for i in range(ends)]),
            cells,
            lax.ppermute(head, axis, [(i + 1, i) for i in range(ends)]),
        ],
        axis=dim,
    )


def attend_kernel(groups, own_ref, *refs):
    others = refs[: groups - 1]
    wq, wk, wv, wo, mixed_ref = refs[groups - 1 :]
    frames, pixels, channels = own_ref.shape
    head_dim = channels // HEADS
    own = own_ref[...].reshape(frames * pixels, channels)
    queries = jnp.dot(own, wq[...], preferred_element_type=F32).astype(BF16).astype(F32)
    keys, values = [], []
    for ref in (own_ref, *others):
        tokens = ref[...].reshape(frames * pixels, channels)
        k = jnp.dot(tokens, wk[...], preferred_element_type=F32).astype(BF16).astype(F32)
        v = jnp.dot(tokens, wv[...], preferred_element_type=F32).astype(BF16).astype(F32)
        for f in range(frames):
            keys.append(k[f * pixels : (f + 1) * pixels])
            values.append(v[f * pixels : (f + 1) * pixels])
    gather = (
        lax.broadcasted_iota(jnp.int32, (channels, LANES), 0) // head_dim
        == lax.broadcasted_iota(jnp.int32, (channels, LANES), 1)
    ).astype(F32).astype(BF16)
    spread = (
        lax.broadcasted_iota(jnp.int32, (LANES, channels), 1) // head_dim
        == lax.broadcasted_iota(jnp.int32, (LANES, channels), 0)
    ).astype(F32).astype(BF16)
    heads_out = []
    for f in range(frames):
        q = queries[f * pixels : (f + 1) * pixels]
        scores = []
        for k in keys:
            product = q * k
            high = product.astype(BF16)
            low = (product - high.astype(F32)).astype(BF16)
            total = jnp.dot(high, gather, preferred_element_type=F32) + jnp.dot(
                low, gather, preferred_element_type=F32
            )
            scores.append(total / math.sqrt(head_dim))
        top = functools.reduce(jnp.maximum, scores)
        exps = [jnp.exp(s - top) for s in scores]
        denom = functools.reduce(jnp.add, exps)
        acc = None
        for e, v in zip(exps, values):
            weight = (e / denom).astype(BF16)
            term = jnp.dot(weight, spread, preferred_element_type=F32) * v
            acc = term if acc is None else acc + term
        heads_out.append(acc.astype(BF16))
    projected = jnp.dot(jnp.concatenate(heads_out, axis=0), wo[...], preferred_element_type=F32)
    mixed = own.astype(F32) + projected
    mixed_ref[...] = mixed.astype(BF16).reshape(frames, pixels, channels)


def attend(parts, wq, wk, wv, wo):
    frames, pixels, channels = parts[0].shape
    block = min(LANES, pixels)
    token_spec = pl.BlockSpec((frames, block, channels), lambda i: (0, i, 0))
    weight_spec = pl.BlockSpec((channels, channels), lambda i: (0, 0))
    return pl.pallas_call(
        functools.partial(attend_kernel, len(parts)),
        grid=(pixels // block,),
        out_shape=jax.ShapeDtypeStruct(parts[0].shape, BF16),
        in_specs=[token_spec] * len(parts) + [weight_spec] * 4,
        out_specs=token_spec,
    )(*parts, wq, wk, wv, wo)


def bit_count(size):
    return size.bit_length() - 1


def grad_kernel(
    frames_n, tiles_n, taps_side, cols, cot_ref, mixed_ref, out_ref, part, recv, send_sem, recv_sem
):
    _, frames, out_channels, _ = cot_ref.shape
    channels = mixed_ref.shape[2]
    pixels = mixed_ref.shape[1]
    chunks, blocks, block_rows, width = part.shape
    fb, tb = bit_count(frames_n), bit_count(tiles_n)
    tile_bits = [("tile", b) for b in range(tb)]
    frame_bits = [("frame", b) for b in range(fb)]
    first, second, rest = tile_bits[:1], tile_bits[1:2], tile_bits[:1:-1]
    orders = (first + second + frame_bits + rest, first + frame_bits + second + rest)
    here = {"tile": lax.axis_index("tile"), "frame": lax.axis_index("frame")}

    def my_bit(axis, b):
        return lax.rem(here[axis] // (1 << b), 2)

    def partner(axis, b):
        return {axis: here[axis] + (1 - 2 * my_bit(axis, b)) * (1 << b)}

    stages = fb + tb
    barrier = pltpu.get_barrier_semaphore()
    for axis, b in orders[0]:
        pl.semaphore_signal(barrier, inc=1, device_id=partner(axis, b), device_id_type=MESH)
    pl.semaphore_wait(barrier, stages)

    def order_of(k):
        return orders[k % 2]

    def start_of(k, stage):
        total = 0
        for j in range(stage):
            total = total + my_bit(*order_of(k)[j]) * (blocks >> (j + 1))
        return total

    def copy_of(k, stage):
        axis, b = order_of(k)[stage]
        size = blocks >> (stage + 1)
        source = start_of(k, stage) + (1 - my_bit(axis, b)) * size
        return pltpu.make_async_remote_copy(
            src_ref=part.at[k, pl.ds(source, size)],
            dst_ref=recv.at[k, pl.ds(size, size)],
            send_sem=send_sem.at[k, stage],
            recv_sem=recv_sem.at[k, stage],
            device_id=partner(axis, b),
            device_id_type=MESH,
        )

    def compute(k):
        for f in range(frames_n):
            unit = f * chunks + k
            tap, col = (unit * width) // channels, (unit * width) % channels
            row_shift, col_shift = tap // taps_side, tap % taps_side
            lo = (taps_side - 1 - row_shift) * cols
            acc = None
            for g in range(frames):
                term = jnp.dot(
                    cot_ref[col_shift, g, :, lo : lo + pixels],
                    mixed_ref[g, :, col : col + width],
                    preferred_element_type=F32,
                )
                acc = term if acc is None else acc + term
            acc = acc.astype(BF16)
            for t in range(tiles_n):
                at = {"tile": t, "frame": f}
                place = 0
                for j, (axis, b) in enumerate(order_of(k)):
                    place += ((at[axis] >> b) & 1) * (blocks >> (j + 1))
                part[k, place] = acc[t * block_rows : (t + 1) * block_rows]

    def merge(k, stage):
        copy_of(k, stage).wait_recv()
        size = blocks >> (stage + 1)
        mine = start_of(k, stage + 1)
        got = recv[k, size : 2 * size].astype(F32)
        total = part[k, pl.ds(mine, size)].astype(F32) + got
        if stage < stages - 1:
            part[k, pl.ds(mine, size)] = total.astype(BF16)
            copy_of(k, stage + 1).start()
        else:
            out_ref[:, k * width : (k + 1) * width] = total[0]

    for step in range(chunks + stages):
        for stage in range(stages - 1, -1, -1):
            k = step - 1 - stage
            if 0 <= k < chunks:
                merge(k, stage)
        if step < chunks:
            compute(step)
            copy_of(step, 0).start()
    for k in range(chunks):
        for stage in range(stages):
            copy_of(k, stage).wait_send()


def kernel_grad(shifted_cot, mixed, cols):
    frames_n, tiles_n = lax.axis_size("frame"), lax.axis_size("tile")
    taps_side = shifted_cot.shape[0]
    out_channels, channels = shifted_cot.shape[2], mixed.shape[2]
    chunks = taps_side * taps_side
    width = channels // frames_n
    blocks, block_rows = frames_n * tiles_n, out_channels // tiles_n
    stages = bit_count(blocks)
    return pl.pallas_call(
        functools.partial(grad_kernel, frames_n, tiles_n, taps_side, cols),
        out_shape=jax.ShapeDtypeStruct((block_rows, chunks * width), F32),
        in_specs=[pl.BlockSpec(memory_space=pltpu.VMEM)] * 2,
        out_specs=pl.BlockSpec(memory_space=pltpu.VMEM),
        scratch_shapes=[
            pltpu.VMEM((chunks, blocks, block_rows, width), BF16),
            pltpu.VMEM((chunks, blocks, block_rows, width), BF16),
            pltpu.SemaphoreType.DMA((chunks, stages)),
            pltpu.SemaphoreType.DMA((chunks, stages)),
        ],
        compiler_params=pltpu.CompilerParams(
            collective_id=0, has_side_effects=True, vmem_limit_bytes=48 * 1024 * 1024
        ),
    )(shifted_cot, mixed)


def on_device(
    latents, conv_weight, conv_bias, query_weight, key_weight, value_weight, out_weight, cotangent
):
    frames, rows, cols, channels = latents.shape
    count = lax.axis_size("frame")
    padded = with_halo(latents, "tile", 1)
    convolved = lax.conv_general_dilated(
        padded,
        conv_weight,
        (1, 1),
        ((0, 0), (1, 1)),
        dimension_numbers=("NHWC", "HWIO", "NHWC"),
        preferred_element_type=F32,
    )
    hidden = jax.nn.silu(convolved + conv_bias).astype(BF16).reshape(frames, rows * cols, channels)
    parts = [hidden] + [
        lax.ppermute(hidden, "frame", [(i, (i + k) % count) for i in range(count)])
        for k in range(1, count)
    ]
    mixed = attend(parts, query_weight, key_weight, value_weight, out_weight)
    turned = with_halo(cotangent, "tile", 1).transpose(0, 3, 1, 2)
    side = conv_weight.shape[1]
    wide = jnp.pad(turned, ((0, 0), (0, 0), (0, 0), (1, 1)))
    shifted_cot = jnp.stack(
        [wide[..., side - 1 - s : side - 1 - s + cols] for s in range(side)]
    ).reshape(side, frames, channels, (rows + 2) * cols)
    conv_grad = kernel_grad(shifted_cot, mixed, cols)
    return (mixed.reshape(frames, rows, cols, channels), conv_grad)


def solution(mesh):
    in_specs = (
        P("frame", "tile", None, None),
        P(),
        P(),
        P(),
        P(),
        P(),
        P(),
        P("frame", "tile", None, None),
    )
    out_specs = (P("frame", "tile", None, None), P("tile", "frame"))
    return jax.shard_map(
        on_device, mesh=mesh, in_specs=in_specs, out_specs=out_specs, check_vma=False
    )
```

time: 292 us -> 138 us (0.47)
  waiting for transfers between devices: 165 us -> 9.45 us
  Pallas kernels: 0 us -> 77.9 us
  blocking collectives: 28.8 us -> 0 us
  local copies, waits for them, and re-layouts: 34.6 us -> 14.7 us
  between operations: 14.5 us -> 0.79 us
  matrix products: 29.5 us -> 17.8 us
  other arithmetic: 10.1 us -> 5.19 us
    unnamed x3 -> x0, waiting for transfers between devices: 118 us -> none
    pallas_call x0 -> x2, Pallas kernels: none -> 77.9 us  [the longest x1 66.2 us: kernel_grad(): pl.pallas_call(functools.partial(grad_kernel, frames_n, tiles_n, taps_sid...]
    reduce_scatter x1 -> x0, waiting for transfers between devices: 34.6 us -> none  [on_device(): lax.psum_scatter(partial_grad, 'frame', scatter_dimension=1, tiled=True)]
    all_to_all x2 -> x0, blocking collectives: 28.8 us -> none  [the longest x1 14.9 us: on_device(): lax.all_to_all(pixel_mixed, 'frame', split_axis=0, concat_axis=2, tiled=T...]
    dot_general x7 -> x0, matrix products: 23.7 us -> none  [the longest x1 7.55 us: on_device(): lax.dot_general(flat_cot, patches, (((0,), (0,)), ((), ())), preferred_el...]
    conv_general_dilated x1, matrix products: 5.76 us -> 17.8 us  [on_device(): lax.conv_general_dilated(padded, conv_weight, (1, 1), ((0, 0), (1, 1)), d...]
    unnamed x31 -> x12, local copies, waits for them, and re-layouts: 18.2 us -> 6.77 us
    reshape x3 -> x0, local copies, waits for them, and re-layouts: 6.98 us -> none  [the longest x1 2.79 us: on_device(): values = values.reshape(shaped)]
  transfers between devices with their start and end apart: 6 -> 5, of which waited for: 4 -> 2; matrix products, arithmetic and copies ran while one was open for 0% -> 22% of each run, Pallas kernels for 0% -> 0%
where the time goes in v1:
time: 138 us
  Pallas kernels  77.9 us (56%)
  matrix products  17.8 us (13%)
  local copies, waits for them, and re-layouts  14.7 us (11%)
  starting transfers between devices  11.8 us (9%)
  waiting for transfers between devices  9.45 us (7%)
  other arithmetic  5.19 us (4%)
    pallas_call x1, Pallas kernels, kernel_grad(): pl.pallas_call(functools.partial(grad_kernel, frames_n, tiles_n, taps_sid...  66.2 us
    conv_general_dilated x1, matrix products, on_device(): lax.conv_general_dilated(padded, conv_weight, (1, 1), ((0, 0), (1, 1)), d...  17.8 us
    pallas_call x1, Pallas kernels, attend(): pl.pallas_call(functools.partial(attend_kernel, len(parts)), grid=(pixels...  11.7 us
    ppermute x2, starting transfers between devices, with_halo(): lax.ppermute(tail, axis, [(i, i + 1) for i in range(ends)])  7.57 us
    unnamed x12, local copies, waits for them, and re-layouts  6.77 us
    another operation x3, local copies, waits for them, and re-layouts, on_device(): jnp.stack([wide[..., side - 1 - s:side - 1 - s + cols] for s in range(sid...  5 us
    ppermute x2, waiting for transfers between devices, with_halo(): lax.ppermute(head, axis, [(i + 1, i) for i in range(ends)])  4.79 us
    ppermute x1, waiting for transfers between devices, on_device(): lax.ppermute(hidden, 'frame', [(i, (i + k) % count) for i in range(count)])  4.66 us
  transfers between devices with their start and end apart: 5, of which 2 were waited for; matrix products, arithmetic and copies ran while one was open for 22% of the time, Pallas kernels for 0%

profile of v1, /device:TPU:0, one launch (start us, length us, event | category | flops | bytes accessed | tf_op | source)
XLA Modules:
  0.0 137.6 jit_solution(7102211204287374589)
XLA Ops:
  0.6 0.0 copy-start.2
  0.6 2.4 %copy.24 = bf16[2,4,128,512]{3,0,2,1:T(2,128)(2,1)S(1)} copy(bf16[2,4,128,512]{3,2,1,0:T(8,128)(2,1)} %param.8) | data formatting | bytes 2097152 | tf_op args[0]
  3.0 0.4 fusion.3
  3.4 2.4 %collective-permute-start = (bf16[2,1,128,512]{3,0,2,1:T(2,128)(2,1)S(1)}, bf16[2,1,128,512]{3,0,2,1:T(2,128)(2,1)S(1)}, u32[]{:S(2)}, u32[]{:S(2)}) collective-permute-start(bf16[2,1,128,512]{3,0,2,1:T(2,128)(2,1)S(1)} %get-tuple-element.6), channel_id=1, source_target_pairs={{0,1},{1,2},{2,3},{3,4},{4,5},{5,6},{6,7},{7,8},{8,9},{9,10},{10,1... | collective-permute-start | bytes 786440 | tf_op jit(solution)/shard_map/ppermute | solution.py:25
  5.8 1.3 collective-permute-start.1
  7.1 0.0 copy-done.2
  7.2 0.0 copy-start.3
  7.2 5.2 %collective-permute-start.3 = (bf16[2,1,128,512]{3,2,1,0:T(8,128)(2,1)S(1)}, bf16[2,1,128,512]{3,2,1,0:T(8,128)(2,1)S(1)}, u32[]{:S(2)}, u32[]{:S(2)}) collective-permute-start(bf16[2,1,128,512]{3,2,1,0:T(8,128)(2,1)S(1)} %get-tuple-element.5), channel_id=1, source_target_pairs={{0,1},{1,2},{2,3},{3,4},{4,5},{5,6},{6,7},{7,8},{8,9},{9,10},{10,1... | collective-permute-start | bytes 786440 | tf_op jit(solution)/shard_map/ppermute | solution.py:25
  12.4 0.0 collective-permute-done
  12.4 0.0 collective-permute-done.1
  12.4 17.8 %fusion = f32[2,4,128,512]{3,0,2,1:T(2,128)S(1)} fusion(bf16[3,3,512,512]{3,2,1,0:T(8,128)(2,1)} %param.9, bf16[2,1,128,512]{3,0,2,1:T(2,128)(2,1)S(1)} %collective-permute-done.1, bf16[2,4,128,512]{3,0,2,1:T(2,128)(2,1)S(1)} %copy.24, bf16[2,1,128,512]{3,0,2,1:T(2,128)(2,1)S(1)} %collective-permute-done), kind=kOutput, calls=%fused_computation.4 | convolution fusion | flops 4811390976 | bytes 8388608 | tf_op jit(solution)/shard_map/conv_general_dilated | solution.py:226
  30.2 0.0 copy-done.3
  30.2 1.7 %multiply_convert_fusion = bf16[2,4,128,512]{3,2,1,0:T(8,128)(2,1)} fusion(f32[2,4,128,512]{3,0,2,1:T(2,128)S(1)} %fusion, f32[512]{0:T(512)S(1)} %copy-done.3), kind=kLoop, calls=%fused_computation.2 | loop fusion | flops 3145728 | bytes 3147776 | tf_op jit(solution)/shard_map/convert_element_type | solution.py:234
  31.8 1.5 %collective-permute-start.2 = (bf16[2,512,512]{2,1,0:T(8,128)(2,1)}, bf16[2,512,512]{2,1,0:T(8,128)(2,1)}, u32[]{:S(2)}, u32[]{:S(2)}) collective-permute-start(bf16[2,512,512]{2,1,0:T(8,128)(2,1)} %bitcast.own_ref), channel_id=1, source_target_pairs={{0,16},{16,0},{1,17},{17,1},{2,18},{18,2},{3,19},{19,3},{4,20},{20... | collective-permute-start | bytes 3145736 | tf_op jit(solution)/shard_map/ppermute | solution.py:236
  33.3 1.5 %collective-permute-start.4 = (bf16[2,1,128,512]{3,2,1,0:T(8,128)(2,1)S(1)}, bf16[2,1,128,512]{3,2,1,0:T(8,128)(2,1)S(1)}, u32[]{:S(2)}, u32[]{:S(2)}) collective-permute-start(bf16[2,1,128,512]{3,2,1,0:T(8,128)(2,1)S(1)} %get-tuple-element.4), channel_id=1, source_target_pairs={{1,0},{2,1},{3,2},{4,3},{5,4},{6,5},{7,6},{8,7},{9,8},{10,9},{11,1... | collective-permute-start | bytes 786440 | tf_op jit(solution)/shard_map/ppermute | solution.py:27
  34.8 0.0 collective-permute-done.3
  34.8 0.1 constant_dynamic-update-slice_fusion.1
  34.9 4.8 %collective-permute-done.4 = bf16[2,1,128,512]{3,2,1,0:T(8,128)(2,1)S(1)} collective-permute-done((bf16[2,1,128,512]{3,2,1,0:T(8,128)(2,1)S(1)}, bf16[2,1,128,512]{3,2,1,0:T(8,128)(2,1)S(1)}, u32[]{:S(2)}, u32[]{:S(2)}) %collective-permute-start.4) | collective-permute-done | bytes 262176 | tf_op jit(solution)/shard_map/ppermute | solution.py:27
  39.7 0.7 copy.29
  40.4 2.5 %pad_slice_fusion.1 = (bf16[2,512,6,128]{1,3,2,0:T(8,128)(2,1)}, bf16[2,512,6,128]{1,3,2,0:T(8,128)(2,1)}) fusion(bf16[2,512,6,128]{1,3,2,0:T(8,128)(2,1)S(1)} %bitcast.10), kind=kLoop, calls=%fused_computation.6 | loop fusion | bytes 4718592 | tf_op jit(solution)/shard_map/slice | solution.py:244
  42.9 1.7 %copy.28 = bf16[1,2,512,768]{3,2,1,0:T(8,128)(2,1)S(1)} copy(bf16[1,2,512,768]{2,3,1,0:T(8,128)(2,1)} %bitcast.12) | data formatting | bytes 3145728 | tf_op jit(solution)/shard_map/stack | solution.py:243
  44.6 2.6 %copy.30 = bf16[1,2,512,768]{3,2,1,0:T(8,128)(2,1)} copy(bf16[1,2,512,768]{2,3,1,0:T(8,128)(2,1)} %bitcast.11) | data formatting | bytes 3145728 | tf_op jit(solution)/shard_map/stack | solution.py:243
  47.2 3.5 %pad_maximum_fusion.cot_ref = bf16[3,2,512,768]{3,2,1,0:T(8,128)(2,1)} fusion(bf16[1,2,512,768]{3,2,1,0:T(8,128)(2,1)} %copy.30, bf16[1,2,512,768]{3,2,1,0:T(8,128)(2,1)S(1)} %copy.29, bf16[1,2,512,768]{3,2,1,0:T(8,128)(2,1)S(1)} %copy.28), kind=kLoop, calls=%fused_computation | loop fusion | flops 4718592 | bytes 9437184 | tf_op jit(solution)/shard_map/stack | solution.py:243
  50.8 4.7 %collective-permute-done.2.refs_0_ = bf16[2,512,512]{2,1,0:T(8,128)(2,1)} collective-permute-done((bf16[2,512,512]{2,1,0:T(8,128)(2,1)}, bf16[2,512,512]{2,1,0:T(8,128)(2,1)}, u32[]{:S(2)}, u32[]{:S(2)}) %collective-permute-start.2) | collective-permute-done | bytes 1048608 | tf_op jit(solution)/shard_map/ppermute | solution.py:236
  55.4 11.7 %shard_map.95.mixed_ref = bf16[2,512,512]{2,1,0:T(8,128)(2,1)} custom-call(bf16[2,512,512]{2,1,0:T(8,128)(2,1)} %bitcast.own_ref, bf16[2,512,512]{2,1,0:T(8,128)(2,1)} %collective-permute-done.2.refs_0_, bf16[512,512]{1,0:T(8,128)(2,1)} %refs_1_.1, bf16[512,512]{1,0:T(8,128)(2,1)} %refs_2_.1, bf16[512,512]{1,0:T(8,128)(2,1)} %refs_3_.1, bf16[512,512]{1,0:T(8,128)(2,1)} %refs_4_.1), custom_call_target="tpu_custom_call" | custom-call | tf_op jit(solution)/shard_map/pallas_call | solution.py:87
  67.1 0.0 copy-start
  67.1 2.3 %copy-done = bf16[3,2,512,768]{3,2,1,0:T(8,128)(2,1)S(1)} copy-done((bf16[3,2,512,768]{3,2,1,0:T(8,128)(2,1)S(1)}, bf16[3,2,512,768]{3,2,1,0:T(8,128)(2,1)}, u32[]{:S(2)}) %copy-start) | copy-done | bytes 4718616
  69.5 0.0 copy-start.1
  69.5 1.2 copy-done.1
  70.7 66.2 %shard_map.96 = f32[32,2304]{1,0:T(8,128)S(1)} custom-call(bf16[3,2,512,768]{3,2,1,0:T(8,128)(2,1)S(1)} %copy-done, bf16[2,512,512]{2,1,0:T(8,128)(2,1)S(1)} %copy-done.1), custom_call_target="tpu_custom_call" | custom-call | tf_op jit(solution)/shard_map/pallas_call | solution.py:203
  136.9 0.7 copy.37
  (3 shorter events, 0.1 us)
Async XLA Ops:
  0.6 6.5 %copy-start.2 = (bf16[2,4,128,512]{3,2,1,0:T(8,128)(2,1)S(1)}, bf16[2,4,128,512]{3,2,1,0:T(8,128)(2,1)}, u32[]{:S(2)}) copy-start(bf16[2,4,128,512]{3,2,1,0:T(8,128)(2,1)} %param.15) | copy-start | bytes 3145732
  3.4 9.0 %collective-permute-start = (bf16[2,1,128,512]{3,0,2,1:T(2,128)(2,1)S(1)}, bf16[2,1,128,512]{3,0,2,1:T(2,128)(2,1)S(1)}, u32[]{:S(2)}, u32[]{:S(2)}) collective-permute-start(bf16[2,1,128,512]{3,0,2,1:T(2,128)(2,1)S(1)} %get-tuple-element.6), channel_id=1, source_target_pairs={{0,1},{1,2},{2,3},{3,4},{4,5},{5,6},{6,7},{7,8},{8,9},{9,10},{10,1... | collective-permute-start | bytes 786440 | tf_op jit(solution)/shard_map/ppermute | solution.py:25
  5.8 6.5 %collective-permute-start.1 = (bf16[2,1,128,512]{3,0,2,1:T(2,128)(2,1)S(1)}, bf16[2,1,128,512]{3,0,2,1:T(2,128)(2,1)S(1)}, u32[]{:S(2)}, u32[]{:S(2)}) collective-permute-start(bf16[2,1,128,512]{3,0,2,1:T(2,128)(2,1)S(1)} %get-tuple-element.7), channel_id=1, source_target_pairs={{1,0},{2,1},{3,2},{4,3},{5,4},{6,5},{7,6},{8,7},{9,8},{10,9},{11,1... | collective-permute-start | bytes 786440 | tf_op jit(solution)/shard_map/ppermute | solution.py:27
  7.2 23.0 %copy-start.3 = (f32[512]{0:T(512)S(1)}, f32[512]{0:T(512)}, u32[]{:S(2)}) copy-start(f32[512]{0:T(512)} %param.10) | copy-start | bytes 6148
  7.2 27.6 %collective-permute-start.3 = (bf16[2,1,128,512]{3,2,1,0:T(8,128)(2,1)S(1)}, bf16[2,1,128,512]{3,2,1,0:T(8,128)(2,1)S(1)}, u32[]{:S(2)}, u32[]{:S(2)}) collective-permute-start(bf16[2,1,128,512]{3,2,1,0:T(8,128)(2,1)S(1)} %get-tuple-element.5), channel_id=1, source_target_pairs={{0,1},{1,2},{2,3},{3,4},{4,5},{5,6},{6,7},{7,8},{8,9},{9,10},{10,1... | collective-permute-start | bytes 786440 | tf_op jit(solution)/shard_map/ppermute | solution.py:25
  31.8 23.6 %collective-permute-start.2 = (bf16[2,512,512]{2,1,0:T(8,128)(2,1)}, bf16[2,512,512]{2,1,0:T(8,128)(2,1)}, u32[]{:S(2)}, u32[]{:S(2)}) collective-permute-start(bf16[2,512,512]{2,1,0:T(8,128)(2,1)} %bitcast.own_ref), channel_id=1, source_target_pairs={{0,16},{16,0},{1,17},{17,1},{2,18},{18,2},{3,19},{19,3},{4,20},{20... | collective-permute-start | bytes 3145736 | tf_op jit(solution)/shard_map/ppermute | solution.py:236
  33.3 6.4 %collective-permute-start.4 = (bf16[2,1,128,512]{3,2,1,0:T(8,128)(2,1)S(1)}, bf16[2,1,128,512]{3,2,1,0:T(8,128)(2,1)S(1)}, u32[]{:S(2)}, u32[]{:S(2)}) collective-permute-start(bf16[2,1,128,512]{3,2,1,0:T(8,128)(2,1)S(1)} %get-tuple-element.4), channel_id=1, source_target_pairs={{1,0},{2,1},{3,2},{4,3},{5,4},{6,5},{7,6},{8,7},{9,8},{10,9},{11,1... | collective-permute-start | bytes 786440 | tf_op jit(solution)/shard_map/ppermute | solution.py:27
  67.1 2.3 %copy-start = (bf16[3,2,512,768]{3,2,1,0:T(8,128)(2,1)S(1)}, bf16[3,2,512,768]{3,2,1,0:T(8,128)(2,1)}, u32[]{:S(2)}) copy-start(bf16[3,2,512,768]{3,2,1,0:T(8,128)(2,1)} %pad_maximum_fusion.cot_ref) | copy-start | bytes 14155780
  69.5 1.2 copy-start.1

commit v2 on v1

--- a/solution.py
+++ b/solution.py
@@ -97,6 +97,13 @@
     return size.bit_length() - 1
 
 
+def split_bits(frames_n, tiles_n):
+    tile_bits = [("tile", b) for b in range(bit_count(tiles_n))]
+    frame_bits = [("frame", b) for b in range(bit_count(frames_n))]
+    first, second, rest = tile_bits[:1], tile_bits[1:2], tile_bits[2:]
+    return (first + second + frame_bits, first + frame_bits + second), rest
+
+
 def grad_kernel(
     frames_n, tiles_n, taps_side, cols, cot_ref, mixed_ref, out_ref, part, recv, send_sem, recv_sem
 ):
@@ -104,11 +111,9 @@
     channels = mixed_ref.shape[2]
     pixels = mixed_ref.shape[1]
     chunks, blocks, block_rows, width = part.shape
-    fb, tb = bit_count(frames_n), bit_count(tiles_n)
-    tile_bits = [("tile", b) for b in range(tb)]
-    frame_bits = [("frame", b) for b in range(fb)]
-    first, second, rest = tile_bits[:1], tile_bits[1:2], tile_bits[:1:-1]
-    orders = (first + second + frame_bits + rest, first + frame_bits + second + rest)
+    orders, rest = split_bits(frames_n, tiles_n)
+    halvings = len(orders[0])
+    group = 1 << len(rest)
     here = {"tile": lax.axis_index("tile"), "frame": lax.axis_index("frame")}
 
     def my_bit(axis, b):
@@ -117,11 +122,21 @@
     def partner(axis, b):
         return {axis: here[axis] + (1 - 2 * my_bit(axis, b)) * (1 << b)}
 
-    stages = fb + tb
+    def flipped(mask):
+        tile, place = here["tile"], 0
+        for j, (axis, b) in enumerate(rest):
+            bit = my_bit(axis, b)
+            turned = 1 - bit if (mask >> j) & 1 else bit
+            tile = tile + (turned - bit) * (1 << b)
+            place = place + turned * (1 << j)
+        return {"tile": tile}, place
+
     barrier = pltpu.get_barrier_semaphore()
-    for axis, b in orders[0]:
-        pl.semaphore_signal(barrier, inc=1, device_id=partner(axis, b), device_id_type=MESH)
-    pl.semaphore_wait(barrier, stages)
+    friends = [partner(axis, b) for axis, b in orders[0]]
+    friends += [flipped(mask)[0] for mask in range(1, group)]
+    for friend in friends:
+        pl.semaphore_signal(barrier, inc=1, device_id=friend, device_id_type=MESH)
+    pl.semaphore_wait(barrier, len(friends))
 
     def order_of(k):
         return orders[k % 2]
@@ -132,18 +147,29 @@
             total = total + my_bit(*order_of(k)[j]) * (blocks >> (j + 1))
         return total
 
-    def copy_of(k, stage):
-        axis, b = order_of(k)[stage]
-        size = blocks >> (stage + 1)
-        source = start_of(k, stage) + (1 - my_bit(axis, b)) * size
-        return pltpu.make_async_remote_copy(
-            src_ref=part.at[k, pl.ds(source, size)],
-            dst_ref=recv.at[k, pl.ds(size, size)],
-            send_sem=send_sem.at[k, stage],
-            recv_sem=recv_sem.at[k, stage],
-            device_id=partner(axis, b),
-            device_id_type=MESH,
-        )
+    def copies_of(k, stage):
+        if stage < halvings:
+            axis, b = order_of(k)[stage]
+            size = blocks >> (stage + 1)
+            source = start_of(k, stage) + (1 - my_bit(axis, b)) * size
+            todo = [(source, size, size, stage, partner(axis, b))]
+        else:
+            base = start_of(k, halvings)
+            todo = []
+            for mask in range(1, group):
+                device, place = flipped(mask)
+                todo.append((base + place, 1, mask, halvings + mask - 1, device))
+        return [
+            pltpu.make_async_remote_copy(
+                src_ref=part.at[k, pl.ds(source, size)],
+                dst_ref=recv.at[k, pl.ds(target, size)],
+                send_sem=send_sem.at[k, sem],
+                recv_sem=recv_sem.at[k, sem],
+                device_id=device,
+                device_id_type=MESH,
+            )
+            for source, size, target, sem, device in todo
+        ]
 
     def compute(k):
         for f in range(frames_n):
@@ -165,31 +191,41 @@
                 place = 0
                 for j, (axis, b) in enumerate(order_of(k)):
                     place += ((at[axis] >> b) & 1) * (blocks >> (j + 1))
+                for j, (axis, b) in enumerate(rest):
+                    place += ((at[axis] >> b) & 1) << j
                 part[k, place] = acc[t * block_rows : (t + 1) * block_rows]
 
     def merge(k, stage):
-        copy_of(k, stage).wait_recv()
-        size = blocks >> (stage + 1)
-        mine = start_of(k, stage + 1)
-        got = recv[k, size : 2 * size].astype(F32)
-        total = part[k, pl.ds(mine, size)].astype(F32) + got
-        if stage < stages - 1:
+        for copy in copies_of(k, stage):
+            copy.wait_recv()
+        if stage < halvings:
+            size = blocks >> (stage + 1)
+            mine = start_of(k, stage + 1)
+            got = recv[k, size : 2 * size].astype(F32)
+            total = part[k, pl.ds(mine, size)].astype(F32) + got
             part[k, pl.ds(mine, size)] = total.astype(BF16)
-            copy_of(k, stage + 1).start()
+            for copy in copies_of(k, stage + 1):
+                copy.start()
         else:
-            out_ref[:, k * width : (k + 1) * width] = total[0]
-
-    for step in range(chunks + stages):
-        for stage in range(stages - 1, -1, -1):
-            k = step - 1 - stage
+            total = part[k, start_of(k, halvings) + flipped(0)[1]].astype(F32)
+            for mask in range(1, group):
+                total = total + recv[k, mask].astype(F32)
+            out_ref[:, k * width : (k + 1) * width] = total
+
+    due = [2, 5] + [7 + 2 * j for j in range(halvings - 2)] + [7 + 2 * (halvings - 2)]
+    for step in range(chunks + due[halvings]):
+        for stage in range(halvings, -1, -1):
+            k = step - due[stage]
             if 0 <= k < chunks:
                 merge(k, stage)
         if step < chunks:
             compute(step)
-            copy_of(step, 0).start()
+            for copy in copies_of(step, 0):
+                copy.start()
     for k in range(chunks):
-        for stage in range(stages):
-            copy_of(k, stage).wait_send()
+        for stage in range(halvings + 1):
+            for copy in copies_of(k, stage):
+                copy.wait_send()
 
 
 def kernel_grad(shifted_cot, mixed, cols):
@@ -199,7 +235,8 @@
     chunks = taps_side * taps_side
     width = channels // frames_n
     blocks, block_rows = frames_n * tiles_n, out_channels // tiles_n
-    stages = bit_count(blocks)
+    orders, rest = split_bits(frames_n, tiles_n)
+    stages = len(orders[0]) + (1 << len(rest)) - 1
     return pl.pallas_call(
         functools.partial(grad_kernel, frames_n, tiles_n, taps_side, cols),
         out_shape=jax.ShapeDtypeStruct((block_rows, chunks * width), F32),

time: 138 us -> 113 us (0.82)
  Pallas kernels: 77.9 us -> 53 us
    pallas_call x1, Pallas kernels: 66.2 us -> 41.3 us  [kernel_grad(): pl.pallas_call(functools.partial(grad_kernel, frames_n, tiles_n, taps_sid...]
  transfers between devices with their start and end apart: 5 -> 5, of which waited for: 2 -> 2; matrix products, arithmetic and copies ran while one was open for 22% -> 27% of each run, Pallas kernels for 0% -> 0%
where the time goes in v2:
time: 113 us
  Pallas kernels  53 us (47%)
  matrix products  17.8 us (16%)
  local copies, waits for them, and re-layouts  14.7 us (13%)
  starting transfers between devices  11.8 us (10%)
  waiting for transfers between devices  9.45 us (8%)
  other arithmetic  5.19 us (5%)
    pallas_call x1, Pallas kernels, kernel_grad(): pl.pallas_call(functools.partial(grad_kernel, frames_n, tiles_n, taps_sid...  41.3 us
    conv_general_dilated x1, matrix products, on_device(): lax.conv_general_dilated(padded, conv_weight, (1, 1), ((0, 0), (1, 1)), d...  17.8 us
    pallas_call x1, Pallas kernels, attend(): pl.pallas_call(functools.partial(attend_kernel, len(parts)), grid=(pixels...  11.7 us
    ppermute x2, starting transfers between devices, with_halo(): lax.ppermute(tail, axis, [(i, i + 1) for i in range(ends)])  7.57 us
    unnamed x12, local copies, waits for them, and re-layouts  6.77 us
    another operation x3, local copies, waits for them, and re-layouts, on_device(): jnp.stack([wide[..., side - 1 - s:side - 1 - s + cols] for s in range(sid...  5 us
    ppermute x2, waiting for transfers between devices, with_halo(): lax.ppermute(head, axis, [(i + 1, i) for i in range(ends)])  4.79 us
    ppermute x1, waiting for transfers between devices, on_device(): lax.ppermute(hidden, 'frame', [(i, (i + k) % count) for i in range(count)])  4.66 us
  transfers between devices with their start and end apart: 5, of which 2 were waited for; matrix products, arithmetic and copies ran while one was open for 27% of the time, Pallas kernels for 0%

profile of v2, /device:TPU:0, one launch (start us, length us, event | category | flops | bytes accessed | tf_op | source)
XLA Modules:
  0.0 112.7 jit_solution(2422235391346378729)
XLA Ops:
  0.6 0.0 copy-start.2
  0.6 2.4 %copy.24 = bf16[2,4,128,512]{3,0,2,1:T(2,128)(2,1)S(1)} copy(bf16[2,4,128,512]{3,2,1,0:T(8,128)(2,1)} %param.8) | data formatting | bytes 2097152 | tf_op args[0]
  3.0 0.4 fusion.3
  3.4 2.4 %collective-permute-start = (bf16[2,1,128,512]{3,0,2,1:T(2,128)(2,1)S(1)}, bf16[2,1,128,512]{3,0,2,1:T(2,128)(2,1)S(1)}, u32[]{:S(2)}, u32[]{:S(2)}) collective-permute-start(bf16[2,1,128,512]{3,0,2,1:T(2,128)(2,1)S(1)} %get-tuple-element.6), channel_id=1, source_target_pairs={{0,1},{1,2},{2,3},{3,4},{4,5},{5,6},{6,7},{7,8},{8,9},{9,10},{10,1... | collective-permute-start | bytes 786440 | tf_op jit(solution)/shard_map/ppermute | solution.py:25
  5.8 1.3 %collective-permute-start.1 = (bf16[2,1,128,512]{3,0,2,1:T(2,128)(2,1)S(1)}, bf16[2,1,128,512]{3,0,2,1:T(2,128)(2,1)S(1)}, u32[]{:S(2)}, u32[]{:S(2)}) collective-permute-start(bf16[2,1,128,512]{3,0,2,1:T(2,128)(2,1)S(1)} %get-tuple-element.7), channel_id=1, source_target_pairs={{1,0},{2,1},{3,2},{4,3},{5,4},{6,5},{7,6},{8,7},{9,8},{10,9},{11,1... | collective-permute-start | bytes 786440 | tf_op jit(solution)/shard_map/ppermute | solution.py:27
  7.1 0.0 copy-done.2
  7.2 0.0 copy-start.3
  7.2 5.2 %collective-permute-start.3 = (bf16[2,1,128,512]{3,2,1,0:T(8,128)(2,1)S(1)}, bf16[2,1,128,512]{3,2,1,0:T(8,128)(2,1)S(1)}, u32[]{:S(2)}, u32[]{:S(2)}) collective-permute-start(bf16[2,1,128,512]{3,2,1,0:T(8,128)(2,1)S(1)} %get-tuple-element.5), channel_id=1, source_target_pairs={{0,1},{1,2},{2,3},{3,4},{4,5},{5,6},{6,7},{7,8},{8,9},{9,10},{10,1... | collective-permute-start | bytes 786440 | tf_op jit(solution)/shard_map/ppermute | solution.py:25
  12.4 0.0 collective-permute-done
  12.4 0.0 collective-permute-done.1
  12.4 17.8 %fusion = f32[2,4,128,512]{3,0,2,1:T(2,128)S(1)} fusion(bf16[3,3,512,512]{3,2,1,0:T(8,128)(2,1)} %param.9, bf16[2,1,128,512]{3,0,2,1:T(2,128)(2,1)S(1)} %collective-permute-done.1, bf16[2,4,128,512]{3,0,2,1:T(2,128)(2,1)S(1)} %copy.24, bf16[2,1,128,512]{3,0,2,1:T(2,128)(2,1)S(1)} %collective-permute-done), kind=kOutput, calls=%fused_computation.4 | convolution fusion | flops 4811390976 | bytes 8388608 | tf_op jit(solution)/shard_map/conv_general_dilated | solution.py:263
  30.2 0.0 copy-done.3
  30.2 1.7 %multiply_convert_fusion = bf16[2,4,128,512]{3,2,1,0:T(8,128)(2,1)} fusion(f32[2,4,128,512]{3,0,2,1:T(2,128)S(1)} %fusion, f32[512]{0:T(512)S(1)} %copy-done.3), kind=kLoop, calls=%fused_computation.2 | loop fusion | flops 3145728 | bytes 3147776 | tf_op jit(solution)/shard_map/convert_element_type | solution.py:271
  31.8 1.5 %collective-permute-start.2 = (bf16[2,512,512]{2,1,0:T(8,128)(2,1)}, bf16[2,512,512]{2,1,0:T(8,128)(2,1)}, u32[]{:S(2)}, u32[]{:S(2)}) collective-permute-start(bf16[2,512,512]{2,1,0:T(8,128)(2,1)} %bitcast.own_ref), channel_id=1, source_target_pairs={{0,16},{16,0},{1,17},{17,1},{2,18},{18,2},{3,19},{19,3},{4,20},{20... | collective-permute-start | bytes 3145736 | tf_op jit(solution)/shard_map/ppermute | solution.py:273
  33.3 1.5 %collective-permute-start.4 = (bf16[2,1,128,512]{3,2,1,0:T(8,128)(2,1)S(1)}, bf16[2,1,128,512]{3,2,1,0:T(8,128)(2,1)S(1)}, u32[]{:S(2)}, u32[]{:S(2)}) collective-permute-start(bf16[2,1,128,512]{3,2,1,0:T(8,128)(2,1)S(1)} %get-tuple-element.4), channel_id=1, source_target_pairs={{1,0},{2,1},{3,2},{4,3},{5,4},{6,5},{7,6},{8,7},{9,8},{10,9},{11,1... | collective-permute-start | bytes 786440 | tf_op jit(solution)/shard_map/ppermute | solution.py:27
  34.8 0.0 collective-permute-done.3
  34.8 0.1 constant_dynamic-update-slice_fusion.1
  34.9 4.8 %collective-permute-done.4 = bf16[2,1,128,512]{3,2,1,0:T(8,128)(2,1)S(1)} collective-permute-done((bf16[2,1,128,512]{3,2,1,0:T(8,128)(2,1)S(1)}, bf16[2,1,128,512]{3,2,1,0:T(8,128)(2,1)S(1)}, u32[]{:S(2)}, u32[]{:S(2)}) %collective-permute-start.4) | collective-permute-done | bytes 262176 | tf_op jit(solution)/shard_map/ppermute | solution.py:27
  39.7 0.7 copy.29
  40.4 2.5 %pad_slice_fusion.1 = (bf16[2,512,6,128]{1,3,2,0:T(8,128)(2,1)}, bf16[2,512,6,128]{1,3,2,0:T(8,128)(2,1)}) fusion(bf16[2,512,6,128]{1,3,2,0:T(8,128)(2,1)S(1)} %bitcast.10), kind=kLoop, calls=%fused_computation.6 | loop fusion | bytes 4718592 | tf_op jit(solution)/shard_map/slice | solution.py:281
  42.9 1.7 %copy.28 = bf16[1,2,512,768]{3,2,1,0:T(8,128)(2,1)S(1)} copy(bf16[1,2,512,768]{2,3,1,0:T(8,128)(2,1)} %bitcast.12) | data formatting | bytes 3145728 | tf_op jit(solution)/shard_map/stack | solution.py:280
  44.6 2.6 %copy.30 = bf16[1,2,512,768]{3,2,1,0:T(8,128)(2,1)} copy(bf16[1,2,512,768]{2,3,1,0:T(8,128)(2,1)} %bitcast.11) | data formatting | bytes 3145728 | tf_op jit(solution)/shard_map/stack | solution.py:280
  47.2 3.5 %pad_maximum_fusion.cot_ref = bf16[3,2,512,768]{3,2,1,0:T(8,128)(2,1)} fusion(bf16[1,2,512,768]{3,2,1,0:T(8,128)(2,1)} %copy.30, bf16[1,2,512,768]{3,2,1,0:T(8,128)(2,1)S(1)} %copy.29, bf16[1,2,512,768]{3,2,1,0:T(8,128)(2,1)S(1)} %copy.28), kind=kLoop, calls=%fused_computation | loop fusion | flops 4718592 | bytes 9437184 | tf_op jit(solution)/shard_map/stack | solution.py:280
  50.8 4.7 %collective-permute-done.2.refs_0_ = bf16[2,512,512]{2,1,0:T(8,128)(2,1)} collective-permute-done((bf16[2,512,512]{2,1,0:T(8,128)(2,1)}, bf16[2,512,512]{2,1,0:T(8,128)(2,1)}, u32[]{:S(2)}, u32[]{:S(2)}) %collective-permute-start.2) | collective-permute-done | bytes 1048608 | tf_op jit(solution)/shard_map/ppermute | solution.py:273
  55.4 11.7 %shard_map.95.mixed_ref = bf16[2,512,512]{2,1,0:T(8,128)(2,1)} custom-call(bf16[2,512,512]{2,1,0:T(8,128)(2,1)} %bitcast.own_ref, bf16[2,512,512]{2,1,0:T(8,128)(2,1)} %collective-permute-done.2.refs_0_, bf16[512,512]{1,0:T(8,128)(2,1)} %refs_1_.1, bf16[512,512]{1,0:T(8,128)(2,1)} %refs_2_.1, bf16[512,512]{1,0:T(8,128)(2,1)} %refs_3_.1, bf16[512,512]{1,0:T(8,128)(2,1)} %refs_4_.1), custom_call_target="tpu_custom_call" | custom-call | tf_op jit(solution)/shard_map/pallas_call | solution.py:87
  67.1 0.0 copy-start
  67.1 2.3 %copy-done = bf16[3,2,512,768]{3,2,1,0:T(8,128)(2,1)S(1)} copy-done((bf16[3,2,512,768]{3,2,1,0:T(8,128)(2,1)S(1)}, bf16[3,2,512,768]{3,2,1,0:T(8,128)(2,1)}, u32[]{:S(2)}) %copy-start) | copy-done | bytes 4718616
  69.5 0.0 copy-start.1
  69.5 1.2 %copy-done.1 = bf16[2,512,512]{2,1,0:T(8,128)(2,1)S(1)} copy-done((bf16[2,512,512]{2,1,0:T(8,128)(2,1)S(1)}, bf16[2,512,512]{2,1,0:T(8,128)(2,1)}, u32[]{:S(2)}) %copy-start.1) | copy-done | bytes 1048600
  70.7 41.3 %shard_map.96 = f32[32,2304]{1,0:T(8,128)S(1)} custom-call(bf16[3,2,512,768]{3,2,1,0:T(8,128)(2,1)S(1)} %copy-done, bf16[2,512,512]{2,1,0:T(8,128)(2,1)S(1)} %copy-done.1), custom_call_target="tpu_custom_call" | custom-call | tf_op jit(solution)/shard_map/pallas_call | solution.py:240
  112.0 0.7 copy.37
  (3 shorter events, 0.1 us)
Async XLA Ops:
  0.6 6.5 %copy-start.2 = (bf16[2,4,128,512]{3,2,1,0:T(8,128)(2,1)S(1)}, bf16[2,4,128,512]{3,2,1,0:T(8,128)(2,1)}, u32[]{:S(2)}) copy-start(bf16[2,4,128,512]{3,2,1,0:T(8,128)(2,1)} %param.15) | copy-start | bytes 3145732
  3.4 9.0 %collective-permute-start = (bf16[2,1,128,512]{3,0,2,1:T(2,128)(2,1)S(1)}, bf16[2,1,128,512]{3,0,2,1:T(2,128)(2,1)S(1)}, u32[]{:S(2)}, u32[]{:S(2)}) collective-permute-start(bf16[2,1,128,512]{3,0,2,1:T(2,128)(2,1)S(1)} %get-tuple-element.6), channel_id=1, source_target_pairs={{0,1},{1,2},{2,3},{3,4},{4,5},{5,6},{6,7},{7,8},{8,9},{9,10},{10,1... | collective-permute-start | bytes 786440 | tf_op jit(solution)/shard_map/ppermute | solution.py:25
  5.8 6.5 %collective-permute-start.1 = (bf16[2,1,128,512]{3,0,2,1:T(2,128)(2,1)S(1)}, bf16[2,1,128,512]{3,0,2,1:T(2,128)(2,1)S(1)}, u32[]{:S(2)}, u32[]{:S(2)}) collective-permute-start(bf16[2,1,128,512]{3,0,2,1:T(2,128)(2,1)S(1)} %get-tuple-element.7), channel_id=1, source_target_pairs={{1,0},{2,1},{3,2},{4,3},{5,4},{6,5},{7,6},{8,7},{9,8},{10,9},{11,1... | collective-permute-start | bytes 786440 | tf_op jit(solution)/shard_map/ppermute | solution.py:27
  7.2 23.0 %copy-start.3 = (f32[512]{0:T(512)S(1)}, f32[512]{0:T(512)}, u32[]{:S(2)}) copy-start(f32[512]{0:T(512)} %param.10) | copy-start | bytes 6148
  7.2 27.6 %collective-permute-start.3 = (bf16[2,1,128,512]{3,2,1,0:T(8,128)(2,1)S(1)}, bf16[2,1,128,512]{3,2,1,0:T(8,128)(2,1)S(1)}, u32[]{:S(2)}, u32[]{:S(2)}) collective-permute-start(bf16[2,1,128,512]{3,2,1,0:T(8,128)(2,1)S(1)} %get-tuple-element.5), channel_id=1, source_target_pairs={{0,1},{1,2},{2,3},{3,4},{4,5},{5,6},{6,7},{7,8},{8,9},{9,10},{10,1... | collective-permute-start | bytes 786440 | tf_op jit(solution)/shard_map/ppermute | solution.py:25
  31.8 23.6 %collective-permute-start.2 = (bf16[2,512,512]{2,1,0:T(8,128)(2,1)}, bf16[2,512,512]{2,1,0:T(8,128)(2,1)}, u32[]{:S(2)}, u32[]{:S(2)}) collective-permute-start(bf16[2,512,512]{2,1,0:T(8,128)(2,1)} %bitcast.own_ref), channel_id=1, source_target_pairs={{0,16},{16,0},{1,17},{17,1},{2,18},{18,2},{3,19},{19,3},{4,20},{20... | collective-permute-start | bytes 3145736 | tf_op jit(solution)/shard_map/ppermute | solution.py:273
  33.3 6.4 %collective-permute-start.4 = (bf16[2,1,128,512]{3,2,1,0:T(8,128)(2,1)S(1)}, bf16[2,1,128,512]{3,2,1,0:T(8,128)(2,1)S(1)}, u32[]{:S(2)}, u32[]{:S(2)}) collective-permute-start(bf16[2,1,128,512]{3,2,1,0:T(8,128)(2,1)S(1)} %get-tuple-element.4), channel_id=1, source_target_pairs={{1,0},{2,1},{3,2},{4,3},{5,4},{6,5},{7,6},{8,7},{9,8},{10,9},{11,1... | collective-permute-start | bytes 786440 | tf_op jit(solution)/shard_map/ppermute | solution.py:27
  67.1 2.3 %copy-start = (bf16[3,2,512,768]{3,2,1,0:T(8,128)(2,1)S(1)}, bf16[3,2,512,768]{3,2,1,0:T(8,128)(2,1)}, u32[]{:S(2)}) copy-start(bf16[3,2,512,768]{3,2,1,0:T(8,128)(2,1)} %pad_maximum_fusion.cot_ref) | copy-start | bytes 14155780
  69.5 1.2 %copy-start.1 = (bf16[2,512,512]{2,1,0:T(8,128)(2,1)S(1)}, bf16[2,512,512]{2,1,0:T(8,128)(2,1)}, u32[]{:S(2)}) copy-start(bf16[2,512,512]{2,1,0:T(8,128)(2,1)} %shard_map.95.mixed_ref) | copy-start | bytes 3145732

commit v3 on v2

--- a/solution.py
+++ b/solution.py
@@ -15,31 +15,14 @@
 BF16 = jnp.bfloat16
 
 
-def with_halo(cells, axis, dim):
-    count = lax.axis_size(axis)
-    ends = count - 1
-    head = lax.slice_in_dim(cells, 0, 1, axis=dim)
-    tail = lax.slice_in_dim(cells, cells.shape[dim] - 1, cells.shape[dim], axis=dim)
-    return jnp.concatenate(
-        [
-            lax.ppermute(tail, axis, [(i, i + 1) for i in range(ends)]),
-            cells,
-            lax.ppermute(head, axis, [(i + 1, i) for i in range(ends)]),
-        ],
-        axis=dim,
-    )
-
-
-def attend_kernel(groups, own_ref, *refs):
-    others = refs[: groups - 1]
-    wq, wk, wv, wo, mixed_ref = refs[groups - 1 :]
-    frames, pixels, channels = own_ref.shape
+def attend(token_parts, wq, wk, wv, wo, frames):
+    own = token_parts[0]
+    channels = own.shape[1]
+    pixels = own.shape[0] // frames
     head_dim = channels // HEADS
-    own = own_ref[...].reshape(frames * pixels, channels)
     queries = jnp.dot(own, wq[...], preferred_element_type=F32).astype(BF16).astype(F32)
     keys, values = [], []
-    for ref in (own_ref, *others):
-        tokens = ref[...].reshape(frames * pixels, channels)
+    for tokens in token_parts:
         k = jnp.dot(tokens, wk[...], preferred_element_type=F32).astype(BF16).astype(F32)
         v = jnp.dot(tokens, wv[...], preferred_element_type=F32).astype(BF16).astype(F32)
         for f in range(frames):
@@ -76,21 +59,186 @@
         heads_out.append(acc.astype(BF16))
     projected = jnp.dot(jnp.concatenate(heads_out, axis=0), wo[...], preferred_element_type=F32)
     mixed = own.astype(F32) + projected
-    mixed_ref[...] = mixed.astype(BF16).reshape(frames, pixels, channels)
-
-
-def attend(parts, wq, wk, wv, wo):
-    frames, pixels, channels = parts[0].shape
-    block = min(LANES, pixels)
-    token_spec = pl.BlockSpec((frames, block, channels), lambda i: (0, i, 0))
-    weight_spec = pl.BlockSpec((channels, channels), lambda i: (0, 0))
+    return mixed.astype(BF16)
+
+
+def front_kernel(
+    lat_ref, conv_ref, bias_ref, wq, wk, wv, wo, cot_ref,
+    mixed_ref, turned_ref,
+    lat_rim, cot_rim, moved, hidden, others,
+    rim_send, rim_recv, hid_send, hid_recv,
+):
+    frames, rows, cols, channels = lat_ref.shape
+    side = conv_ref.shape[0]
+    count, tiles = lax.axis_size("frame"), lax.axis_size("tile")
+    frame, tile = lax.axis_index("frame"), lax.axis_index("tile")
+    has = (tile > 0, tile < tiles - 1)
+    beside = (tile - 1, tile + 1)
+
+    barrier = pltpu.get_barrier_semaphore()
+    for step in (1, tiles - 1):
+        pl.semaphore_signal(
+            barrier, inc=1, device_id={"tile": lax.rem(tile + step, tiles)}, device_id_type=MESH
+        )
+    for k in range(1, count):
+        pl.semaphore_signal(
+            barrier, inc=1, device_id={"frame": lax.rem(frame + k, count)}, device_id_type=MESH
+        )
+    pl.semaphore_wait(barrier, 2 + count - 1)
+
+    def rim_copy(which, end):
+        source, target = ((lat_ref, lat_rim), (cot_ref, cot_rim))[which]
+        return pltpu.make_async_remote_copy(
+            src_ref=source.at[:, (rows - 1) * end],
+            dst_ref=target.at[1 - end],
+            send_sem=rim_send.at[which, end],
+            recv_sem=rim_recv.at[which, 1 - end],
+            device_id={"tile": beside[end]},
+            device_id_type=MESH,
+        )
+
+    def rim_arrival(which, end):
+        source, target = ((lat_ref, lat_rim), (cot_ref, cot_rim))[which]
+        return pltpu.make_async_remote_copy(
+            src_ref=source.at[:, (rows - 1) * end],
+            dst_ref=target.at[end],
+            send_sem=rim_send.at[which, end],
+            recv_sem=rim_recv.at[which, end],
+            device_id={"tile": beside[end]},
+            device_id_type=MESH,
+        )
+
+    for which in range(2):
+        for end in range(2):
+
+            @pl.when(has[end])
+            def _():
+                rim_copy(which, end).start()
+
+    def settle(which):
+        target = (lat_rim, cot_rim)[which]
+        for end in range(2):
+
+            @pl.when(has[end])
+            def _():
+                rim_arrival(which, end).wait_recv()
+
+            @pl.when(jnp.logical_not(has[end]))
+            def _():
+                target[end] = jnp.zeros_like(target[end])
+
+    def by_column(value, offset):
+        if offset == 0:
+            return value
+        wide = value.astype(F32)
+        rolled = pltpu.roll(wide, (-offset) % cols, 0)
+        at = lax.broadcasted_iota(jnp.int32, wide.shape, 0)
+        edge = 0 if offset < 0 else cols - 1
+        return jnp.where(at == edge, 0.0, rolled).astype(BF16)
+
+    def place(value, f, row):
+        for s in range(side):
+            moved[s, f, row] = by_column(value, s - 1)
+
+    def convolve(row):
+        acc = jnp.broadcast_to(bias_ref[...], (frames * cols, channels))
+        for r in range(side):
+            for s in range(side):
+                acc = acc + jnp.dot(
+                    moved[s, :, row + r].reshape(frames * cols, channels),
+                    conv_ref[r, s],
+                    preferred_element_type=F32,
+                )
+        result = acc / (1.0 + jnp.exp(-acc))
+        hidden[row] = result.astype(BF16)
+        for k in range(1, count):
+            hidden_copy(k, row).start()
+
+    def hidden_copy(k, row):
+        return pltpu.make_async_remote_copy(
+            src_ref=hidden.at[row],
+            dst_ref=others.at[k - 1, row],
+            send_sem=hid_send.at[k - 1, row],
+            recv_sem=hid_recv.at[k - 1, row],
+            device_id={"frame": lax.rem(frame + k, count)},
+            device_id_type=MESH,
+        )
+
+    for row in range(rows):
+        for f in range(frames):
+            place(lat_ref[f, row], f, row + 1)
+    for row in range(1, rows - 1):
+        convolve(row)
+    settle(0)
+    for f in range(frames):
+        place(lat_rim[0, f], f, 0)
+        place(lat_rim[1, f], f, rows + 1)
+    for row in (rows - 1, 0):
+        convolve(row)
+
+    def turn(value, f, row):
+        for s in range(side):
+            turned_ref[s, f, :, row * cols : (row + 1) * cols] = by_column(value, 1 - s).T
+
+    for row in range(rows):
+        for f in range(frames):
+            turn(cot_ref[f, row], f, row + 1)
+    settle(1)
+    for f in range(frames):
+        turn(cot_rim[0, f], f, 0)
+        turn(cot_rim[1, f], f, rows + 1)
+
+    def attend_row(i, carry):
+        row = lax.rem(i + 1, rows)
+        for k in range(1, count):
+            hidden_copy(k, row).wait_recv()
+        parts = [hidden[row]] + [others[k - 1, row] for k in range(1, count)]
+        mixed = attend(parts, wq, wk, wv, wo, frames)
+        for f in range(frames):
+            mixed_ref[f, pl.ds(pl.multiple_of(row * cols, cols), cols)] = mixed[
+                f * cols : (f + 1) * cols
+            ]
+        return carry
+
+    lax.fori_loop(0, rows, attend_row, 0)
+    for row in range(rows):
+        for k in range(1, count):
+            hidden_copy(k, row).wait_send()
+    for which in range(2):
+        for end in range(2):
+
+            @pl.when(has[end])
+            def _():
+                rim_copy(which, end).wait_send()
+
+
+def front(latents, conv_weight, conv_bias, wq, wk, wv, wo, cotangent):
+    frames, rows, cols, channels = latents.shape
+    side = conv_weight.shape[0]
+    count = lax.axis_size("frame")
     return pl.pallas_call(
-        functools.partial(attend_kernel, len(parts)),
-        grid=(pixels // block,),
-        out_shape=jax.ShapeDtypeStruct(parts[0].shape, BF16),
-        in_specs=[token_spec] * len(parts) + [weight_spec] * 4,
-        out_specs=token_spec,
-    )(*parts, wq, wk, wv, wo)
+        front_kernel,
+        out_shape=[
+            jax.ShapeDtypeStruct((frames, rows * cols, channels), BF16),
+            jax.ShapeDtypeStruct((side, frames, channels, (rows + 2) * cols), BF16),
+        ],
+        in_specs=[pl.BlockSpec(memory_space=pltpu.VMEM)] * 8,
+        out_specs=[pl.BlockSpec(memory_space=pltpu.VMEM)] * 2,
+        scratch_shapes=[
+            pltpu.VMEM((2, frames, cols, channels), BF16),
+            pltpu.VMEM((2, frames, cols, channels), BF16),
+            pltpu.VMEM((side, frames, rows + 2, cols, channels), BF16),
+            pltpu.VMEM((rows, frames * cols, channels), BF16),
+            pltpu.VMEM((count - 1, rows, frames * cols, channels), BF16),
+            pltpu.SemaphoreType.DMA((2, 2)),
+            pltpu.SemaphoreType.DMA((2, 2)),
+            pltpu.SemaphoreType.DMA((count - 1, rows)),
+            pltpu.SemaphoreType.DMA((count - 1, rows)),
+        ],
+        compiler_params=pltpu.CompilerParams(
+            collective_id=1, has_side_effects=True, vmem_limit_bytes=56 * 1024 * 1024
+        ),
+    )(latents, conv_weight, conv_bias.reshape(1, -1), wq, wk, wv, wo, cotangent)
 
 
 def bit_count(size):
@@ -258,28 +406,9 @@
     latents, conv_weight, conv_bias, query_weight, key_weight, value_weight, out_weight, cotangent
 ):
     frames, rows, cols, channels = latents.shape
-    count = lax.axis_size("frame")
-    padded = with_halo(latents, "tile", 1)
-    convolved = lax.conv_general_dilated(
-        padded,
-        conv_weight,
-        (1, 1),
-        ((0, 0), (1, 1)),
-        dimension_numbers=("NHWC", "HWIO", "NHWC"),
-        preferred_element_type=F32,
+    mixed, shifted_cot = front(
+        latents, conv_weight, conv_bias, query_weight, key_weight, value_weight, out_weight, cotangent
     )
-    hidden = jax.nn.silu(convolved + conv_bias).astype(BF16).reshape(frames, rows * cols, channels)
-    parts = [hidden] + [
-        lax.ppermute(hidden, "frame", [(i, (i + k) % count) for i in range(count)])
-        for k in range(1, count)
-    ]
-    mixed = attend(parts, query_weight, key_weight, value_weight, out_weight)
-    turned = with_halo(cotangent, "tile", 1).transpose(0, 3, 1, 2)
-    side = conv_weight.shape[1]
-    wide = jnp.pad(turned, ((0, 0), (0, 0), (0, 0), (1, 1)))
-    shifted_cot = jnp.stack(
-        [wide[..., side - 1 - s : side - 1 - s + cols] for s in range(side)]
-    ).reshape(side, frames, channels, (rows + 2) * cols)
     conv_grad = kernel_grad(shifted_cot, mixed, cols)
     return (mixed.reshape(frames, rows, cols, channels), conv_grad)
 

time: 113 us -> 79.6 us (0.70)
  Pallas kernels: 53 us -> 73.5 us
  matrix products: 17.8 us -> 0 us
  starting transfers between devices: 11.8 us -> 0 us
  local copies, waits for them, and re-layouts: 14.7 us -> 5.24 us
  waiting for transfers between devices: 9.45 us -> 0 us
  other arithmetic: 5.19 us -> 0 us
    pallas_call x1, Pallas kernels: 11.7 us -> 38 us  [front(): pl.pallas_call(front_kernel, out_shape=[jax.ShapeDtypeStruct((frames, row...]
    conv_general_dilated x1 -> x0, matrix products: 17.8 us -> none  [on_device(): lax.conv_general_dilated(padded, conv_weight, (1, 1), ((0, 0), (1, 1)), d...]
    ppermute x5 -> x0, starting transfers between devices: 11.8 us -> none  [the longest x2 7.57 us: with_halo(): lax.ppermute(tail, axis, [(i, i + 1) for i in range(ends)])]
    ppermute x5 -> x0, waiting for transfers between devices: 9.45 us -> none  [the longest x2 4.79 us: with_halo(): lax.ppermute(head, axis, [(i + 1, i) for i in range(ends)])]
    pallas_call x1, Pallas kernels: 41.3 us -> 35.5 us  [kernel_grad(): pl.pallas_call(functools.partial(grad_kernel, frames_n, tiles_n, taps_sid...]
    another operation x3 -> x0, local copies, waits for them, and re-layouts: 5 us -> none  [on_device(): jnp.stack([wide[..., side - 1 - s:side - 1 - s + cols] for s in range(sid...]
    another operation x1 -> x0, other arithmetic: 3.53 us -> none  [on_device(): jnp.stack([wide[..., side - 1 - s:side - 1 - s + cols] for s in range(sid...]
    slice x3 -> x0, local copies, waits for them, and re-layouts: 2.9 us -> none  [the longest x1 2.5 us: on_device(): wide[..., side - 1 - s:side - 1 - s + cols]]
  transfers between devices with their start and end apart: 5 -> 0, of which waited for: 2 -> 0; matrix products, arithmetic and copies ran while one was open for 27% -> 0% of each run, Pallas kernels for 0% -> 0%
where the time goes in v3:
time: 79.6 us; the launch traced here: 79.4 us
  Pallas kernels  73.5 us (92%)
  local copies, waits for them, and re-layouts  5.24 us (7%)
    pallas_call x1, Pallas kernels, front(): pl.pallas_call(front_kernel, out_shape=[jax.ShapeDtypeStruct((frames, row...  38 us
    pallas_call x1, Pallas kernels, kernel_grad(): pl.pallas_call(functools.partial(grad_kernel, frames_n, tiles_n, taps_sid...  35.5 us
    unnamed x6, local copies, waits for them, and re-layouts  5.24 us

profile of v3, /device:TPU:0, one launch (start us, length us, event | category | flops | bytes accessed | tf_op | source)
XLA Modules:
  0.0 79.4 jit_solution(244975343816516136)
XLA Ops:
  0.6 38.0 %shard_map.95 = (bf16[2,512,512]{2,1,0:T(8,128)(2,1)}, bf16[3,2,512,768]{3,2,1,0:T(8,128)(2,1)}) custom-call(bf16[2,4,128,512]{3,2,1,0:T(8,128)(2,1)} %lat_ref.1, bf16[3,3,512,512]{3,2,1,0:T(8,128)(2,1)} %conv_ref.1, f32[1,512]{1,0:T(1,128)} %bitcast.3, bf16[512,512]{1,0:T(8,128)(2,1)} %wq.1, bf16[512,512]{1,0:T(8,128)(2,1)} %wk.1, bf16[512,512]{1,0:T(8,128)(2,1)} %wv.1, ...), custom_call_target="tpu_custom_call" | custom-call | tf_op jit(solution)/shard_map/pallas_call | solution.py:219
  38.6 0.0 copy-start
  38.7 2.3 %copy-done = bf16[3,2,512,768]{3,2,1,0:T(8,128)(2,1)S(1)} copy-done((bf16[3,2,512,768]{3,2,1,0:T(8,128)(2,1)S(1)}, bf16[3,2,512,768]{3,2,1,0:T(8,128)(2,1)}, u32[]{:S(2)}) %copy-start) | copy-done | bytes 4718616
  41.0 0.0 copy-start.1
  41.0 1.2 %copy-done.1 = bf16[2,512,512]{2,1,0:T(8,128)(2,1)S(1)} copy-done((bf16[2,512,512]{2,1,0:T(8,128)(2,1)S(1)}, bf16[2,512,512]{2,1,0:T(8,128)(2,1)}, u32[]{:S(2)}) %copy-start.1) | copy-done | bytes 1048600
  42.2 35.5 %shard_map.96 = f32[32,2304]{1,0:T(8,128)S(1)} custom-call(bf16[3,2,512,768]{3,2,1,0:T(8,128)(2,1)S(1)} %copy-done, bf16[2,512,512]{2,1,0:T(8,128)(2,1)S(1)} %copy-done.1), custom_call_target="tpu_custom_call" | custom-call | tf_op jit(solution)/shard_map/pallas_call | solution.py:388
  77.7 1.0 %copy.12 = bf16[2,4,128,512]{3,2,1,0:T(8,128)(2,1)} copy(bf16[2,4,128,512]{3,2,1,0:T(8,128)(2,1)S(1)} %bitcast.2) | data formatting | bytes 2097152
  78.7 0.7 copy.13
Async XLA Ops:
  38.6 2.3 %copy-start = (bf16[3,2,512,768]{3,2,1,0:T(8,128)(2,1)S(1)}, bf16[3,2,512,768]{3,2,1,0:T(8,128)(2,1)}, u32[]{:S(2)}) copy-start(bf16[3,2,512,768]{3,2,1,0:T(8,128)(2,1)} %get-tuple-element.5.cot_ref) | copy-start | bytes 14155780
  41.0 1.2 %copy-start.1 = (bf16[2,512,512]{2,1,0:T(8,128)(2,1)S(1)}, bf16[2,512,512]{2,1,0:T(8,128)(2,1)}, u32[]{:S(2)}) copy-start(bf16[2,512,512]{2,1,0:T(8,128)(2,1)} %get-tuple-element.4.mixed_ref) | copy-start | bytes 3145732

commit v4 on v2

--- a/solution.py
+++ b/solution.py
@@ -1,5 +1,6 @@
 import functools
 import math
+from types import SimpleNamespace
 
 import jax
 import jax.numpy as jnp
@@ -15,31 +16,14 @@
 BF16 = jnp.bfloat16
 
 
-def with_halo(cells, axis, dim):
-    count = lax.axis_size(axis)
-    ends = count - 1
-    head = lax.slice_in_dim(cells, 0, 1, axis=dim)
-    tail = lax.slice_in_dim(cells, cells.shape[dim] - 1, cells.shape[dim], axis=dim)
-    return jnp.concatenate(
-        [
-            lax.ppermute(tail, axis, [(i, i + 1) for i in range(ends)]),
-            cells,
-            lax.ppermute(head, axis, [(i + 1, i) for i in range(ends)]),
-        ],
-        axis=dim,
-    )
-
-
-def attend_kernel(groups, own_ref, *refs):
-    others = refs[: groups - 1]
-    wq, wk, wv, wo, mixed_ref = refs[groups - 1 :]
-    frames, pixels, channels = own_ref.shape
+def attend(token_parts, wq, wk, wv, wo, frames):
+    own = token_parts[0]
+    channels = own.shape[1]
+    pixels = own.shape[0] // frames
     head_dim = channels // HEADS
-    own = own_ref[...].reshape(frames * pixels, channels)
     queries = jnp.dot(own, wq[...], preferred_element_type=F32).astype(BF16).astype(F32)
     keys, values = [], []
-    for ref in (own_ref, *others):
-        tokens = ref[...].reshape(frames * pixels, channels)
+    for tokens in token_parts:
         k = jnp.dot(tokens, wk[...], preferred_element_type=F32).astype(BF16).astype(F32)
         v = jnp.dot(tokens, wv[...], preferred_element_type=F32).astype(BF16).astype(F32)
         for f in range(frames):
@@ -76,21 +60,7 @@
         heads_out.append(acc.astype(BF16))
     projected = jnp.dot(jnp.concatenate(heads_out, axis=0), wo[...], preferred_element_type=F32)
     mixed = own.astype(F32) + projected
-    mixed_ref[...] = mixed.astype(BF16).reshape(frames, pixels, channels)
-
-
-def attend(parts, wq, wk, wv, wo):
-    frames, pixels, channels = parts[0].shape
-    block = min(LANES, pixels)
-    token_spec = pl.BlockSpec((frames, block, channels), lambda i: (0, i, 0))
-    weight_spec = pl.BlockSpec((channels, channels), lambda i: (0, 0))
-    return pl.pallas_call(
-        functools.partial(attend_kernel, len(parts)),
-        grid=(pixels // block,),
-        out_shape=jax.ShapeDtypeStruct(parts[0].shape, BF16),
-        in_specs=[token_spec] * len(parts) + [weight_spec] * 4,
-        out_specs=token_spec,
-    )(*parts, wq, wk, wv, wo)
+    return mixed.astype(BF16)
 
 
 def bit_count(size):
@@ -104,10 +74,9 @@
     return (first + second + frame_bits, first + frame_bits + second), rest
 
 
-def grad_kernel(
-    frames_n, tiles_n, taps_side, cols, cot_ref, mixed_ref, out_ref, part, recv, send_sem, recv_sem
-):
-    _, frames, out_channels, _ = cot_ref.shape
+def reduction_of(taps_side, cols, cot_ref, mixed_ref, out_ref, part, recv, send_sem, recv_sem):
+    frames = cot_ref.shape[1]
+    frames_n, tiles_n = lax.axis_size("frame"), lax.axis_size("tile")
     channels = mixed_ref.shape[2]
     pixels = mixed_ref.shape[1]
     chunks, blocks, block_rows, width = part.shape
@@ -131,13 +100,8 @@
             place = place + turned * (1 << j)
         return {"tile": tile}, place
 
-    barrier = pltpu.get_barrier_semaphore()
     friends = [partner(axis, b) for axis, b in orders[0]]
     friends += [flipped(mask)[0] for mask in range(1, group)]
-    for friend in friends:
-        pl.semaphore_signal(barrier, inc=1, device_id=friend, device_id_type=MESH)
-    pl.semaphore_wait(barrier, len(friends))
-
     def order_of(k):
         return orders[k % 2]
 
@@ -212,75 +176,250 @@
                 total = total + recv[k, mask].astype(F32)
             out_ref[:, k * width : (k + 1) * width] = total
 
-    due = [2, 5] + [7 + 2 * j for j in range(halvings - 2)] + [7 + 2 * (halvings - 2)]
-    for step in range(chunks + due[halvings]):
-        for stage in range(halvings, -1, -1):
-            k = step - due[stage]
-            if 0 <= k < chunks:
-                merge(k, stage)
-        if step < chunks:
-            compute(step)
-            for copy in copies_of(step, 0):
-                copy.start()
-    for k in range(chunks):
-        for stage in range(halvings + 1):
-            for copy in copies_of(k, stage):
-                copy.wait_send()
-
-
-def kernel_grad(shifted_cot, mixed, cols):
-    frames_n, tiles_n = lax.axis_size("frame"), lax.axis_size("tile")
-    taps_side = shifted_cot.shape[0]
-    out_channels, channels = shifted_cot.shape[2], mixed.shape[2]
-    chunks = taps_side * taps_side
-    width = channels // frames_n
-    blocks, block_rows = frames_n * tiles_n, out_channels // tiles_n
-    orders, rest = split_bits(frames_n, tiles_n)
+    def run():
+        due = [2, 5] + [7 + 2 * j for j in range(halvings - 2)] + [7 + 2 * (halvings - 2)]
+        for step in range(chunks + due[halvings]):
+            for stage in range(halvings, -1, -1):
+                k = step - due[stage]
+                if 0 <= k < chunks:
+                    merge(k, stage)
+            if step < chunks:
+                compute(step)
+                for copy in copies_of(step, 0):
+                    copy.start()
+        for k in range(chunks):
+            for stage in range(halvings + 1):
+                for copy in copies_of(k, stage):
+                    copy.wait_send()
+
+    return SimpleNamespace(friends=friends, run=run)
+
+
+def block_kernel(
+    lat_hbm, conv_hbm, bias_ref, wq_hbm, wk_hbm, wv_hbm, wo_hbm, cot_hbm,
+    mixed_hbm, grad_ref,
+    lat_ref, conv_ref, wq, wk, wv, wo, cot_ref, mixed_ref, turned_ref,
+    lat_rim, cot_rim, moved, hidden, others, part, recv,
+    load_sem, rim_send, rim_recv, hid_send, hid_recv, send_sem, recv_sem,
+):
+    frames, rows, cols, channels = lat_hbm.shape
+    side = conv_hbm.shape[0]
+    count, tiles = lax.axis_size("frame"), lax.axis_size("tile")
+    frame, tile = lax.axis_index("frame"), lax.axis_index("tile")
+    has = (tile > 0, tile < tiles - 1)
+    beside = (tile - 1, tile + 1)
+
+    pairs = [
+        (lat_hbm, lat_ref), (conv_hbm, conv_ref), (cot_hbm, cot_ref),
+        (wq_hbm, wq), (wk_hbm, wk), (wv_hbm, wv), (wo_hbm, wo),
+    ]
+    loads = [
+        pltpu.make_async_copy(source, target, load_sem.at[j])
+        for j, (source, target) in enumerate(pairs)
+    ]
+    for load in loads:
+        load.start()
+    reduction = reduction_of(side, cols, turned_ref, mixed_ref, grad_ref, part, recv, send_sem, recv_sem)
+
+    barrier = pltpu.get_barrier_semaphore()
+    greeted = [{"tile": lax.rem(tile + step, tiles)} for step in (1, tiles - 1)]
+    greeted += [{"frame": lax.rem(frame + k, count)} for k in range(1, count)]
+    greeted += reduction.friends
+    for friend in greeted:
+        pl.semaphore_signal(barrier, inc=1, device_id=friend, device_id_type=MESH)
+    pl.semaphore_wait(barrier, len(greeted))
+
+    def rim_copy(which, end):
+        source, target = ((lat_hbm, lat_rim), (cot_hbm, cot_rim))[which]
+        return pltpu.make_async_remote_copy(
+            src_ref=source.at[:, (rows - 1) * end],
+            dst_ref=target.at[1 - end],
+            send_sem=rim_send.at[which, end],
+            recv_sem=rim_recv.at[which, 1 - end],
+            device_id={"tile": beside[end]},
+            device_id_type=MESH,
+        )
+
+    def rim_arrival(which, end):
+        source, target = ((lat_hbm, lat_rim), (cot_hbm, cot_rim))[which]
+        return pltpu.make_async_remote_copy(
+            src_ref=source.at[:, (rows - 1) * end],
+            dst_ref=target.at[end],
+            send_sem=rim_send.at[which, end],
+            recv_sem=rim_recv.at[which, end],
+            device_id={"tile": beside[end]},
+            device_id_type=MESH,
+        )
+
+    for which in range(2):
+        for end in range(2):
+
+            @pl.when(has[end])
+            def _():
+                rim_copy(which, end).start()
+
+    def settle(which):
+        target = (lat_rim, cot_rim)[which]
+        for end in range(2):
+
+            @pl.when(has[end])
+            def _():
+                rim_arrival(which, end).wait_recv()
+
+            @pl.when(jnp.logical_not(has[end]))
+            def _():
+                target[end] = jnp.zeros_like(target[end])
+
+    def by_column(value, offset):
+        if offset == 0:
+            return value
+        wide = value.astype(F32)
+        rolled = pltpu.roll(wide, (-offset) % cols, 0)
+        at = lax.broadcasted_iota(jnp.int32, wide.shape, 0)
+        edge = 0 if offset < 0 else cols - 1
+        return jnp.where(at == edge, 0.0, rolled).astype(BF16)
+
+    def place(value, f, row):
+        for s in range(side):
+            moved[s, f, row] = by_column(value, s - 1)
+
+    def convolve(row):
+        acc = jnp.broadcast_to(bias_ref[...], (frames * cols, channels))
+        for r in range(side):
+            for s in range(side):
+                acc = acc + jnp.dot(
+                    moved[s, :, row + r].reshape(frames * cols, channels),
+                    conv_ref[r, s],
+                    preferred_element_type=F32,
+                )
+        result = acc / (1.0 + jnp.exp(-acc))
+        hidden[row] = result.astype(BF16)
+        for k in range(1, count):
+            hidden_copy(k, row).start()
+
+    def hidden_copy(k, row):
+        return pltpu.make_async_remote_copy(
+            src_ref=hidden.at[row],
+            dst_ref=others.at[k - 1, row],
+            send_sem=hid_send.at[k - 1, row],
+            recv_sem=hid_recv.at[k - 1, row],
+            device_id={"frame": lax.rem(frame + k, count)},
+            device_id_type=MESH,
+        )
+
+    loads[0].wait()
+    for row in range(rows):
+        for f in range(frames):
+            place(lat_ref[f, row], f, row + 1)
+    loads[1].wait()
+    for row in range(1, rows - 1):
+        convolve(row)
+    settle(0)
+    for f in range(frames):
+        place(lat_rim[0, f], f, 0)
+        place(lat_rim[1, f], f, rows + 1)
+    for row in (rows - 1, 0):
+        convolve(row)
+
+    def turn(value, f, row):
+        for s in range(side):
+            turned_ref[s, f, :, row * cols : (row + 1) * cols] = by_column(value, 1 - s).T
+
+    loads[2].wait()
+    for row in range(rows):
+        for f in range(frames):
+            turn(cot_ref[f, row], f, row + 1)
+    settle(1)
+    for f in range(frames):
+        turn(cot_rim[0, f], f, 0)
+        turn(cot_rim[1, f], f, rows + 1)
+
+    for load in loads[3:]:
+        load.wait()
+
+    def attend_row(i, carry):
+        row = lax.rem(i + 1, rows)
+        for k in range(1, count):
+            hidden_copy(k, row).wait_recv()
+        parts = [hidden[row]] + [others[k - 1, row] for k in range(1, count)]
+        mixed = attend(parts, wq, wk, wv, wo, frames)
+        for f in range(frames):
+            mixed_ref[f, pl.ds(pl.multiple_of(row * cols, cols), cols)] = mixed[
+                f * cols : (f + 1) * cols
+            ]
+        return carry
+
+    lax.fori_loop(0, rows, attend_row, 0)
+    store = pltpu.make_async_copy(mixed_ref, mixed_hbm, load_sem.at[0])
+    store.start()
+    reduction.run()
+    store.wait()
+    for row in range(rows):
+        for k in range(1, count):
+            hidden_copy(k, row).wait_send()
+    for which in range(2):
+        for end in range(2):
+
+            @pl.when(has[end])
+            def _():
+                rim_copy(which, end).wait_send()
+
+
+def block(latents, conv_weight, conv_bias, wq, wk, wv, wo, cotangent):
+    frames, rows, cols, channels = latents.shape
+    side = conv_weight.shape[0]
+    out_channels = cotangent.shape[3]
+    count, tiles_n = lax.axis_size("frame"), lax.axis_size("tile")
+    chunks, width = side * side, channels // count
+    blocks, block_rows = count * tiles_n, out_channels // tiles_n
+    orders, rest = split_bits(count, tiles_n)
     stages = len(orders[0]) + (1 << len(rest)) - 1
+    hbm = pl.BlockSpec(memory_space=pltpu.HBM)
+    vmem = pl.BlockSpec(memory_space=pltpu.VMEM)
+    square = pltpu.VMEM((channels, channels), BF16)
     return pl.pallas_call(
-        functools.partial(grad_kernel, frames_n, tiles_n, taps_side, cols),
-        out_shape=jax.ShapeDtypeStruct((block_rows, chunks * width), F32),
-        in_specs=[pl.BlockSpec(memory_space=pltpu.VMEM)] * 2,
-        out_specs=pl.BlockSpec(memory_space=pltpu.VMEM),
+        block_kernel,
+        out_shape=[
+            jax.ShapeDtypeStruct((frames, rows * cols, channels), BF16),
+            jax.ShapeDtypeStruct((block_rows, chunks * width), F32),
+        ],
+        in_specs=[hbm, hbm, vmem] + [hbm] * 5,
+        out_specs=[hbm, vmem],
         scratch_shapes=[
+            pltpu.VMEM(latents.shape, BF16),
+            pltpu.VMEM(conv_weight.shape, BF16),
+            square, square, square, square,
+            pltpu.VMEM(cotangent.shape, BF16),
+            pltpu.VMEM((frames, rows * cols, channels), BF16),
+            pltpu.VMEM((side, frames, out_channels, (rows + 2) * cols), BF16),
+            pltpu.VMEM((2, frames, cols, channels), BF16),
+            pltpu.VMEM((2, frames, cols, channels), BF16),
+            pltpu.VMEM((side, frames, rows + 2, cols, channels), BF16),
+            pltpu.VMEM((rows, frames * cols, channels), BF16),
+            pltpu.VMEM((count - 1, rows, frames * cols, channels), BF16),
             pltpu.VMEM((chunks, blocks, block_rows, width), BF16),
             pltpu.VMEM((chunks, blocks, block_rows, width), BF16),
+            pltpu.SemaphoreType.DMA((7,)),
+            pltpu.SemaphoreType.DMA((2, 2)),
+            pltpu.SemaphoreType.DMA((2, 2)),
+            pltpu.SemaphoreType.DMA((count - 1, rows)),
+            pltpu.SemaphoreType.DMA((count - 1, rows)),
             pltpu.SemaphoreType.DMA((chunks, stages)),
             pltpu.SemaphoreType.DMA((chunks, stages)),
         ],
         compiler_params=pltpu.CompilerParams(
-            collective_id=0, has_side_effects=True, vmem_limit_bytes=48 * 1024 * 1024
+            collective_id=0, has_side_effects=True, vmem_limit_bytes=63 * 1024 * 1024
         ),
-    )(shifted_cot, mixed)
+    )(latents, conv_weight, conv_bias.reshape(1, -1), wq, wk, wv, wo, cotangent)
 
 
 def on_device(
     latents, conv_weight, conv_bias, query_weight, key_weight, value_weight, out_weight, cotangent
 ):
     frames, rows, cols, channels = latents.shape
-    count = lax.axis_size("frame")
-    padded = with_halo(latents, "tile", 1)
-    convolved = lax.conv_general_dilated(
-        padded,
-        conv_weight,
-        (1, 1),
-        ((0, 0), (1, 1)),
-        dimension_numbers=("NHWC", "HWIO", "NHWC"),
-        preferred_element_type=F32,
+    mixed, conv_grad = block(
+        latents, conv_weight, conv_bias, query_weight, key_weight, value_weight, out_weight, cotangent
     )
-    hidden = jax.nn.silu(convolved + conv_bias).astype(BF16).reshape(frames, rows * cols, channels)
-    parts = [hidden] + [
-        lax.ppermute(hidden, "frame", [(i, (i + k) % count) for i in range(count)])
-        for k in range(1, count)
-    ]
-    mixed = attend(parts, query_weight, key_weight, value_weight, out_weight)
-    turned = with_halo(cotangent, "tile", 1).transpose(0, 3, 1, 2)
-    side = conv_weight.shape[1]
-    wide = jnp.pad(turned, ((0, 0), (0, 0), (0, 0), (1, 1)))
-    shifted_cot = jnp.stack(
-        [wide[..., side - 1 - s : side - 1 - s + cols] for s in range(side)]
-    ).reshape(side, frames, channels, (rows + 2) * cols)
-    conv_grad = kernel_grad(shifted_cot, mixed, cols)
     return (mixed.reshape(frames, rows, cols, channels), conv_grad)
 
 

time: 113 us -> 73.3 us (0.65)
  matrix products: 17.8 us -> 0 us
  Pallas kernels: 53 us -> 68.5 us
  starting transfers between devices: 11.8 us -> 0 us
  local copies, waits for them, and re-layouts: 14.7 us -> 3.96 us
  waiting for transfers between devices: 9.45 us -> 0 us
  other arithmetic: 5.19 us -> 0 us
    conv_general_dilated x1 -> x0, matrix products: 17.8 us -> none  [on_device(): lax.conv_general_dilated(padded, conv_weight, (1, 1), ((0, 0), (1, 1)), d...]
    pallas_call x2 -> x1, Pallas kernels: 53 us -> 68.5 us  [block(): pl.pallas_call(block_kernel, out_shape=[jax.ShapeDtypeStruct((frames, row...]
    ppermute x5 -> x0, starting transfers between devices: 11.8 us -> none  [the longest x2 7.57 us: with_halo(): lax.ppermute(tail, axis, [(i, i + 1) for i in range(ends)])]
    ppermute x5 -> x0, waiting for transfers between devices: 9.45 us -> none  [the longest x2 4.79 us: with_halo(): lax.ppermute(head, axis, [(i + 1, i) for i in range(ends)])]
    another operation x3 -> x0, local copies, waits for them, and re-layouts: 5 us -> none  [on_device(): jnp.stack([wide[..., side - 1 - s:side - 1 - s + cols] for s in range(sid...]
    another operation x1 -> x0, other arithmetic: 3.53 us -> none  [on_device(): jnp.stack([wide[..., side - 1 - s:side - 1 - s + cols] for s in range(sid...]
    slice x3 -> x0, local copies, waits for them, and re-layouts: 2.9 us -> none  [the longest x1 2.5 us: on_device(): wide[..., side - 1 - s:side - 1 - s + cols]]
    unnamed x12 -> x2, local copies, waits for them, and re-layouts: 6.77 us -> 3.96 us
  transfers between devices with their start and end apart: 5 -> 0, of which waited for: 2 -> 0; matrix products, arithmetic and copies ran while one was open for 27% -> 0% of each run, Pallas kernels for 0% -> 0%
where the time goes in v4:
time: 73.3 us; the launch traced here: 73.1 us
  Pallas kernels  68.5 us (93%)
  local copies, waits for them, and re-layouts  3.96 us (5%)
    pallas_call x1, Pallas kernels, block(): pl.pallas_call(block_kernel, out_shape=[jax.ShapeDtypeStruct((frames, row...  68.5 us
    unnamed x2, local copies, waits for them, and re-layouts  3.96 us

profile of v4, /device:TPU:0, one launch (start us, length us, event | category | flops | bytes accessed | tf_op | source)
XLA Modules:
  0.0 73.1 jit_solution(5337154359568011350)
XLA Ops:
  0.6 68.5 %shard_map.95 = (bf16[2,512,512]{2,1,0:T(8,128)(2,1)}, f32[32,2304]{1,0:T(8,128)}) custom-call(bf16[2,4,128,512]{3,2,1,0:T(8,128)(2,1)} %lat_hbm.1, bf16[3,3,512,512]{3,2,1,0:T(8,128)(2,1)} %conv_hbm.1, f32[1,512]{1,0:T(1,128)} %bitcast.3, bf16[512,512]{1,0:T(8,128)(2,1)} %wq_hbm.1, bf16[512,512]{1,0:T(8,128)(2,1)} %wk_hbm.1, bf16[512,512]{1,0:T(8,128)(2,1)} %wv_hbm.1, ...), custom_call_target="tpu_custom_call" | custom-call | tf_op jit(solution)/shard_map/pallas_call | solution.py:380
  69.1 2.3 %copy.12 = bf16[2,4,128,512]{3,2,1,0:T(8,128)(2,1)} copy(bf16[2,4,128,512]{3,2,1,0:T(8,128)(2,1)} %bitcast.2) | data formatting | bytes 2097152
  71.4 1.7 %copy.13 = f32[32,2304]{1,0:T(8,128)} copy(f32[32,2304]{1,0:T(8,128)} %get-tuple-element.9) | data formatting | bytes 589824
